TPU v7x, 256 devices: a whole 4x4x8 slice. The times are simulated.
256 devices in a mesh: dp: 64 (over z, y, core), group: 4 (over x).
Axes of the slice: x: 4, y: 4, z: 8, core: 2. Of those that a mesh axis runs over, the one named last changes fastest.
Arguments:
- frames: bfloat16 [4, 36864, 2048], P('group', 'dp'), may hold values from -6 to 6
- lengths: int32 [4, 192], P('group', 'dp'), may hold values from 24 to 192, as said below
- destination: int32 [4, 192], P('group', 'dp'), may hold values from 0 to 63, as said below
- offsets: int32 [4, 192], P('group', 'dp'), may hold values from 0 to 360, as said below
- norm_gain: bfloat16 [2048], P(('dp', 'group')), may hold values from 0.099609375 to 1.8984375
- weight_in: bfloat16 [2048, 4096], P(('dp', 'group')), may hold values from -0.125 to 0.125
- depth_kernel: bfloat16 [2048, 32], P(('dp', 'group')), may hold values from -1 to 1
- post_gain: bfloat16 [2048], P(('dp', 'group')), may hold values from 0.099609375 to 1.8984375
- weight_out: bfloat16 [2048, 2048], P(('dp', 'group')), may hold values from -0.125 to 0.125
Outputs:
- mixed: bfloat16 [4, 24576, 2048], P('group', 'dp')
Inputs may be any that keep to these rules, and one draw needn't show every extreme that they name: `destination`: every device of a group sends exactly one utterance to itself, one to dp index + 1 and one to dp index - 1, both taken modulo 64, within its own group index. `lengths`: every device receives utterances with 384 frames in all; one utterance of each device's receipts has exactly 192 frames; in every group some device's slots are full. `offsets`: the utterances that one device receives lie back to back without gaps or intersection over its 384 rows.
All inputs are finite; a program needn't handle non-finite values.
Results may differ from a plain program's by a relative error of at most 0.0085.
Values may be sent and summed in bfloat16 or wider, within the bound.
A program may use at most 128 MiB of HBM per device.

v0:
```python
import jax
import jax.numpy as jnp
from jax import lax
from jax.sharding import PartitionSpec as P

D = 2048
KERNEL = 32
MAXLEN = 192
RCV_DEV = 384


epsilon = 1e-05


def shifted(array, axis, by):
    peers = lax.axis_size(axis)
    return lax.ppermute(array, axis, [(i, (i + by) % peers) for i in range(peers)])


def sent_together(arrays, axis, dim, along):
    columns = [a.reshape(*a.shape[:along], -1) for a in arrays]
    both = jnp.concatenate(columns, axis=along)
    out, at, done = (lax.all_gather(both, axis, axis=dim, tiled=True), 0, [])
    for a, column in zip(arrays, columns):
        slab = out[..., at : at + column.shape[along]]
        done.append(slab.reshape(*slab.shape[:along], *a.shape[along:]))
        at += column.shape[along]
    return tuple(done)


def layer_norm(values, scale_gain):
    center = values - jnp.mean(values, axis=-1, keepdims=True)
    spread = jnp.mean(center * center, axis=-1, keepdims=True)
    return center * lax.rsqrt(spread + epsilon) * scale_gain.astype(jnp.float32)


def depth_pass(gated_rows, segment, depth_kernel):
    row_count = gated_rows.shape[0]
    margin = KERNEL // 2
    padded = jnp.pad(gated_rows, ((margin, margin), (0, 0)))
    labels = jnp.pad(segment, (margin, margin), constant_values=-1)
    kernel_rows = depth_kernel.astype(jnp.float32)
    depthwise = jnp.zeros_like(gated_rows)
    for column in range(KERNEL):
        inside = (labels[column : column + row_count] == segment)[:, None]
        depthwise = (
            depthwise
            + jnp.where(inside, padded[column : column + row_count], 0.0) * kernel_rows[:, column]
        )
    return depthwise


def conv_module(inputs, segment, params):
    norm_gain, weight_in, depth_kernel, post_gain, weight_out = params
    widths = inputs.shape[1]
    source = inputs.astype(jnp.float32)
    normed = layer_norm(source, norm_gain).astype(jnp.bfloat16)
    projected = jnp.dot(normed, weight_in, preferred_element_type=jnp.float32)
    gated_rows = projected[:, :widths] * jax.nn.sigmoid(projected[:, widths:])
    depthwise = depth_pass(gated_rows, segment, depth_kernel)
    normed_post = layer_norm(depthwise, post_gain)
    active = (normed_post * jax.nn.sigmoid(normed_post)).astype(jnp.bfloat16)
    return (source + jnp.dot(active, weight_out, preferred_element_type=jnp.float32)).astype(
        jnp.bfloat16
    )


def relocate(own_part, next_part, prev_part):
    from_prev = shifted((next_part[0], next_part[1]), "dp", 1)
    from_next = shifted((prev_part[0], prev_part[1]), "dp", -1)
    received = jnp.zeros((RCV_DEV + MAXLEN, D), jnp.bfloat16)
    segment = jnp.zeros((RCV_DEV,), jnp.int32)
    position = jnp.arange(RCV_DEV, dtype=jnp.int32)
    arrivals = (own_part, from_prev, from_next)
    for label_id in range(3):
        frame_rows, meta_data = arrivals[label_id]
        current = lax.dynamic_slice_in_dim(received, meta_data[1], MAXLEN, 0)
        received = lax.dynamic_update_slice_in_dim(received, current + frame_rows, meta_data[1], 0)
        inside = (position >= meta_data[1]) & (position < meta_data[1] + meta_data[0])
        segment = jnp.where(inside, label_id + 1, segment)
    return (received[:RCV_DEV], segment)


def shards(
    frames, lengths, destination, offsets, norm_gain, weight_in, depth_kernel, post_gain, weight_out
):
    dp_count = lax.axis_size("dp")
    params = sent_together(
        (norm_gain, weight_in, depth_kernel, post_gain, weight_out), ("dp", "group"), 0, 1
    )
    my_index = lax.axis_index("dp")
    local_frames = frames[0]
    lengths_here = lengths[0]
    dest_here = destination[0]
    offsets_here = offsets[0]
    starts = jnp.cumsum(lengths_here) - lengths_here
    relative = (dest_here - my_index) % dp_count
    slot_ids = jnp.arange(3, dtype=jnp.int32)

    def pick_entry(values, which):
        return jnp.sum(jnp.where(slot_ids == which, values, 0))

    def slot_of(code):
        return jnp.sum(jnp.where(relative == code, slot_ids, 0))

    chosen = (slot_of(0), slot_of(1), slot_of(dp_count - 1))

    def cut_utterance(source_rows, which):
        start_row = pick_entry(starts, which)
        live_count = pick_entry(lengths_here, which)
        frame_rows = lax.dynamic_slice_in_dim(source_rows, start_row, MAXLEN, 0)
        keep_rows = jnp.arange(MAXLEN, dtype=jnp.int32) < live_count
        kept = jnp.where(keep_rows[:, None], frame_rows, jnp.zeros_like(frame_rows))
        return (kept, jnp.stack([live_count, pick_entry(offsets_here, which)]))

    received, segment = relocate(
        cut_utterance(local_frames, chosen[0]),
        cut_utterance(local_frames, chosen[1]),
        cut_utterance(local_frames, chosen[2]),
    )
    mixed = conv_module(received, segment, params)
    return mixed[None]


def solution(mesh):
    placed = (
        P("group", "dp", None),
        P("group", "dp"),
        P("group", "dp"),
        P("group", "dp"),
        P(("dp", "group")),
        P(("dp", "group"), None),
        P(("dp", "group"), None),
        P(("dp", "group")),
        P(("dp", "group"), None),
    )
    return jax.shard_map(
        shards, mesh=mesh, in_specs=placed, out_specs=P("group", "dp", None), check_vma=False
    )
```

profile of v0, /device:TPU:1, one launch (start us, length us, event | category | flops | bytes accessed | tf_op | source)
XLA Modules:
  0.0 224.5 jit_solution(2925735645479445195)
XLA Ops:
  6.5 0.0 copy-start
  6.5 0.0 all-gather.2.cloned.1.call-start
  6.5 0.8 copy.12
  7.3 0.7 copy.13
  8.0 1.6 concatenate.3
  9.7 0.0 all-gather.2.cloned.1.call-update
  9.7 0.8 reduce-window.9
  10.5 1.4 fusion.77
  11.9 3.2 %select_reduce_fusion = (s32[]{:T(128)}, s32[]{:T(128)}, s32[]{:T(128)}, s32[]{:T(128)}, s32[]{:T(128)}, /*index=5*/s32[]{:T(128)}) fusion(s32[]{:T(128)} %get-tuple-element.48, s32[1,3]{1,0:T(1,128)} %param.10, s32[3,1]{0,1:T(1,128)S(1)} %reduce-window.9, s32[]{:T(128)} %get-tuple-element.49, s32[]{:T(128)} %get-tuple-element.50), kind=kLoop, calls=%fused_computation.202 | loop fusion | flops 42 | bytes 60 | tf_op jit(solution)/shard_map/reduce_sum | solution.py:101
  20.8 0.6 iota_compare_fusion.8
  21.4 1.2 iota_compare_fusion.6
  22.7 3.5 %bitcast_select_fusion = (bf16[192,2048]{1,0:T(8,128)(2,1)}, bf16[192,2048]{1,0:T(8,128)(2,1)S(1)}, bf16[192,2048]{1,0:T(8,128)(2,1)}) fusion(bf16[1,576,2048]{2,1,0:T(8,128)(2,1)} %param.9, s32[]{:T(128)S(6)} %select_n.199, pred[192]{0:T(512)(128)(4,1)S(1)} %get-tuple-element.93, s32[]{:T(128)S(6)} %select_n.183, pred[192]{0:T(512)(128)(4,1)S(1)} %iota_compare_fusion.8, ...), kind=kLoop, calls=%fused_computation.123 | loop fusion | flops 1179648 | bytes 4719180 | tf_op jit(solution)/shard_map/jit(_where)/select_n | solution.py:113
  26.2 2.7 %collective-permute-start.1 = (bf16[192,2048]{1,0:T(8,128)(2,1)}, bf16[192,2048]{1,0:T(8,128)(2,1)}, u32[]{:S(2)}, u32[]{:S(2)}) collective-permute-start(bf16[192,2048]{1,0:T(8,128)(2,1)} %get-tuple-element.55), channel_id=1, source_target_pairs={{0,4},{4,8},{8,12},{12,16},{16,20},{20,24},{24,28},{28,32},{32,36}... | collective-permute-start | bytes 2359304 | tf_op jit(solution)/shard_map/ppermute | solution.py:17
  28.9 0.0 copy-done
  28.9 2.5 %fusion.81 = (s32[]{:T(128)}, s32[]{:T(128)}, s32[]{:T(128)}) fusion(s32[1,3]{1,0:T(1,128)S(1)} %copy-done, s32[]{:T(128)} %get-tuple-element.48, s32[]{:T(128)} %get-tuple-element.49, s32[]{:T(128)} %get-tuple-element.50), kind=kLoop, calls=%fused_computation.194 | loop fusion | flops 24 | bytes 36 | tf_op jit(solution)/shard_map/reduce_sum | solution.py:101
  31.4 2.5 %pad_add_fusion = (s32[2]{0:T(128)S(1)}, s32[2]{0:T(128)S(1)}) fusion(s32[1]{0:T(128)} %bitcast.7, s32[1]{0:T(128)} %bitcast.6, s32[1]{0:T(128)} %bitcast.11, s32[1]{0:T(128)} %bitcast.10), kind=kLoop, calls=%fused_computation.187 | loop fusion | flops 4 | bytes 32 | tf_op jit(solution)/shard_map/stack | solution.py:114
  33.9 0.0 collective-permute-start
  33.9 0.6 collective-permute-start.3
  34.6 6.0 %collective-permute-start.2 = (s32[2]{0:T(128)S(1)}, s32[2]{0:T(128)S(1)}, u32[]{:S(2)}, u32[]{:S(2)}) collective-permute-start(s32[2]{0:T(128)S(1)} %get-tuple-element.92), channel_id=1, source_target_pairs={{0,252},{4,0},{8,4},{12,8},{16,12},{20,16},{24,20},{28,24},{32,28}... | collective-permute-start | bytes 32 | tf_op jit(solution)/shard_map/ppermute | solution.py:17
  43.6 0.3 broadcast_in_dim.287
  43.9 4.0 %dynamic_update_slice.9 = bf16[576,2048]{1,0:T(8,128)(2,1)S(1)} dynamic-update-slice(bf16[576,2048]{1,0:T(8,128)(2,1)S(1)} %broadcast_in_dim.287, bf16[192,2048]{1,0:T(8,128)(2,1)S(1)} %get-tuple-element.54, s32[]{:T(128)S(6)} %select_n.186, s32[]{:T(128)} %constant.47.clone.1) | dynamic-update-slice | bytes 1572868 | tf_op jit(solution)/shard_map/dynamic_update_slice | solution.py:78
  48.0 0.0 collective-permute-done.2
  48.0 0.6 fusion.87
  49.9 0.0 collective-permute-done
  49.9 0.7 fusion.88
  51.9 1.9 select_select_fusion
  53.8 0.1 slice_compare_fusion.30
  53.9 0.1 slice_compare_fusion.29
  54.0 0.1 slice_compare_fusion.27
  58.0 0.1 slice_compare_fusion.28
  58.1 0.0 collective-permute-done.1
  58.1 1.4 dynamic-slice_add_fusion.1
  59.5 4.0 %dynamic_update_slice.10 = bf16[576,2048]{1,0:T(8,128)(2,1)S(1)} dynamic-update-slice(bf16[576,2048]{1,0:T(8,128)(2,1)S(1)} %dynamic_update_slice.9, bf16[192,2048]{1,0:T(8,128)(2,1)S(1)} %dynamic-slice_add_fusion.1, s32[]{:T(128)S(6)} %select_n.190, s32[]{:T(128)} %constant.47.clone.1) | dynamic-update-slice | bytes 1572868 | tf_op jit(solution)/shard_map/dynamic_update_slice | solution.py:78
  63.6 0.0 collective-permute-done.3
  63.6 1.4 dynamic-slice_add_fusion
  65.0 4.0 %dynamic_update_slice.11 = bf16[576,2048]{1,0:T(8,128)(2,1)S(1)} dynamic-update-slice(bf16[576,2048]{1,0:T(8,128)(2,1)S(1)} %dynamic_update_slice.10, bf16[192,2048]{1,0:T(8,128)(2,1)S(1)} %dynamic-slice_add_fusion, s32[]{:T(128)S(6)} %select_n.197, s32[]{:T(128)} %constant.47.clone.1) | dynamic-update-slice | bytes 1572868 | tf_op jit(solution)/shard_map/dynamic_update_slice | solution.py:78
  69.1 0.3 convert_reduce_fusion
  69.4 0.6 fusion.6
  69.9 84.5 %all-gather.2.cloned.1.call-done = bf16[2048,6178]{1,0:T(8,128)(2,1)} async-done(((bf16[8,6178]{1,0:T(8,128)(2,1)}), bf16[2048,6178]{1,0:T(8,128)(2,1)}) %all-gather.2.cloned.1.call-update) | async-done | bytes 25305104 | tf_op jit(solution)/shard_map/all_gather | solution.py:23
  154.4 1.2 slice_convert_fusion
  155.7 10.4 %slice_reduce_fusion.31 = (f32[2048]{0:T(1024)S(1)}, f32[2048]{0:T(1024)S(1)}, f32[2048]{0:T(1024)S(1)}, f32[2048]{0:T(1024)S(1)}, f32[2048]{0:T(1024)S(1)}, /*i...) fusion(f32[2048,32]{1,0:T(8,128)S(1)} %slice_convert_fusion), kind=kLoop, calls=%fused_computation.119 | loop fusion | bytes 311296 | tf_op jit(solution)/shard_map/slice | solution.py:48
  166.1 7.1 %slice_reduce_fusion.30 = (f32[2048]{0:T(1024)S(1)}, f32[2048]{0:T(1024)S(1)}, f32[2048]{0:T(1024)S(1)}, f32[2048]{0:T(1024)S(1)}, f32[2048]{0:T(1024)S(1)}, /*i...) fusion(f32[2048,32]{1,0:T(8,128)S(1)} %slice_convert_fusion), kind=kLoop, calls=%fused_computation.118 | loop fusion | bytes 212992 | tf_op jit(solution)/shard_map/slice | solution.py:48
  173.2 1.8 convert_reduce_fusion.1
  175.0 12.1 %fusion = f32[384,4096]{1,0:T(8,128)S(1)} fusion(bf16[2048,6178]{1,0:T(8,128)(2,1)} %all-gather.2.cloned.1.call-done, f32[2048]{0:T(1024)S(1)} %get-tuple-element.6, f32[384]{0:T(512)S(1)} %add_rsqrt_fusion.1, f32[384]{0:T(512)S(1)} %broadcast_multiply_fusion.1, bf16[576,2048]{1,0:T(8,128)(2,1)S(1)} %dynamic_update_slice.11), kind=kOutput, calls=%fused_computation | convolution fusion | flops 6446383104 | bytes 24653824 | tf_op jit(solution)/shard_map/dot_general | solution.py:58
  187.0 1.0 fusion.13
  188.0 19.7 %fusion.86 = (f32[384]{0:T(512)S(1)}, f32[384,2048]{1,0:T(8,128)S(1)}) fusion(f32[2048]{0:T(1024)S(1)} %get-tuple-element.8, pred[384]{0:T(512)(128)(4,1)S(1)} %get-tuple-element.86, f32[2048]{0:T(1024)S(1)} %get-tuple-element.9, pred[384]{0:T(512)(128)(4,1)S(1)} %get-tuple-element.57, f32[2048]{0:T(1024)S(1)} %get-tuple-element.10, ...), kind=kLoop, calls=%fused_computation.209 | loop fusion | flops 74710656 | bytes 6567040 | tf_op jit(solution)/shard_map/reduce_sum | solution.py:32
  207.7 0.5 multiply_reduce_fusion
  208.2 9.5 %fusion.60 = bf16[1,384,2048]{2,1,0:T(8,128)(2,1)} fusion(bf16[2048,6178]{1,0:T(8,128)(2,1)} %all-gather.2.cloned.1.call-done, f32[384,2048]{1,0:T(8,128)S(1)} %get-tuple-element.52, f32[2048]{0:T(1024)S(1)} %get-tuple-element.5, f32[384]{0:T(512)S(1)} %add_rsqrt_fusion, f32[384]{0:T(512)S(1)} %broadcast_multiply_fusion, ...), kind=kOutput, calls=%fused_computation.80 | convolution fusion | flops 3229876224 | bytes 14691328 | tf_op jit(solution)/shard_map/dot_general | solution.py:63
  (4 shorter events, 0.0 us)
Async XLA Ops:
  6.5 22.3 %copy-start = (s32[1,3]{1,0:T(1,128)S(1)}, s32[1,3]{1,0:T(1,128)}, u32[]{:S(2)}) copy-start(s32[1,3]{1,0:T(1,128)} %param.12) | copy-start | bytes 40
  6.5 147.9 %all-gather.2.cloned.1.call-start = ((), (), s32[]{:S(2)}) async-start(), calls=%async_computation | async-start | bytes 25790464 | tf_op jit(solution)/shard_map/all_gather | solution.py:23
  26.2 31.9 %collective-permute-start.1 = (bf16[192,2048]{1,0:T(8,128)(2,1)}, bf16[192,2048]{1,0:T(8,128)(2,1)}, u32[]{:S(2)}, u32[]{:S(2)}) collective-permute-start(bf16[192,2048]{1,0:T(8,128)(2,1)} %get-tuple-element.55), channel_id=1, source_target_pairs={{0,4},{4,8},{8,12},{12,16},{16,20},{20,24},{24,28},{28,32},{32,36}... | collective-permute-start | bytes 2359304 | tf_op jit(solution)/shard_map/ppermute | solution.py:17
  33.9 16.0 %collective-permute-start = (s32[2]{0:T(128)S(1)}, s32[2]{0:T(128)S(1)}, u32[]{:S(2)}, u32[]{:S(2)}) collective-permute-start(s32[2]{0:T(128)S(1)} %get-tuple-element.91), channel_id=1, source_target_pairs={{0,4},{4,8},{8,12},{12,16},{16,20},{20,24},{24,28},{28,32},{32,36}... | collective-permute-start | bytes 32 | tf_op jit(solution)/shard_map/ppermute | solution.py:17
  33.9 29.7 %collective-permute-start.3 = (bf16[192,2048]{1,0:T(8,128)(2,1)}, bf16[192,2048]{1,0:T(8,128)(2,1)}, u32[]{:S(2)}, u32[]{:S(2)}) collective-permute-start(bf16[192,2048]{1,0:T(8,128)(2,1)} %get-tuple-element.53), channel_id=1, source_target_pairs={{0,252},{4,0},{8,4},{12,8},{16,12},{20,16},{24,20},{28,24},{32,28}... | collective-permute-start | bytes 2359304 | tf_op jit(solution)/shard_map/ppermute | solution.py:17
  34.6 13.4 %collective-permute-start.2 = (s32[2]{0:T(128)S(1)}, s32[2]{0:T(128)S(1)}, u32[]{:S(2)}, u32[]{:S(2)}) collective-permute-start(s32[2]{0:T(128)S(1)} %get-tuple-element.92), channel_id=1, source_target_pairs={{0,252},{4,0},{8,4},{12,8},{16,12},{20,16},{24,20},{28,24},{32,28}... | collective-permute-start | bytes 32 | tf_op jit(solution)/shard_map/ppermute | solution.py:17
Sparse Core Ops, SparseCore 0:
  11.1 143.2 all-gather.1
where the time goes:
time: 225 us; the launch traced here: 224 us
  waiting for transfers between devices  84.5 us (38%)
  other arithmetic  45.9 us (20%)
  local copies, waits for them, and re-layouts  34.4 us (15%)
  between operations  28.8 us (13%)
  matrix products  21.5 us (10%)
  starting transfers between devices  9.37 us (4%)
    all_gather x1, waiting for transfers between devices, sent_together(): out, at, done = (lax.all_gather(both, axis, axis=dim, tiled=True), 0, [])  84.5 us
    reduce_sum x2, other arithmetic, layer_norm(): center = values - jnp.mean(values, axis=-1, keepdims=True)  20 us
    slice x2, local copies, waits for them, and re-layouts, depth_pass(): kernel_rows[:, column]  17.5 us
    dynamic_update_slice x3, local copies, waits for them, and re-layouts, relocate(): lax.dynamic_update_slice_in_dim(received, current + frame_rows, meta_data...  12.1 us
    dot_general x1, matrix products, conv_module(): projected = jnp.dot(normed, weight_in, preferred_element_type=jnp.float32)  12.1 us
    dot_general x1, matrix products, conv_module(): jnp.dot(active, weight_out, preferred_element_type=jnp.float32)  9.46 us
    ppermute x4, starting transfers between devices, shifted(): lax.ppermute(array, axis, [(i, (i + by) % peers) for i in range(peers)])  9.37 us
    reduce_sum x2, other arithmetic, pick_entry(): return jnp.sum(jnp.where(slot_ids == which, values, 0))  5.76 us
  transfers between devices with their start and end apart: 5, of which 1 were waited for; matrix products, arithmetic and copies ran while one was open for 16% of the time, Pallas kernels for 0%

commit v1 on v0

--- a/solution.py
+++ b/solution.py
@@ -7,6 +7,8 @@
 KERNEL = 32
 MAXLEN = 192
 RCV_DEV = 384
+IN_CHUNKS = 4
+OUT_CHUNKS = 2
 
 
 epsilon = 1e-05
@@ -17,29 +19,17 @@
     return lax.ppermute(array, axis, [(i, (i + by) % peers) for i in range(peers)])
 
 
-def sent_together(arrays, axis, dim, along):
-    columns = [a.reshape(*a.shape[:along], -1) for a in arrays]
-    both = jnp.concatenate(columns, axis=along)
-    out, at, done = (lax.all_gather(both, axis, axis=dim, tiled=True), 0, [])
-    for a, column in zip(arrays, columns):
-        slab = out[..., at : at + column.shape[along]]
-        done.append(slab.reshape(*slab.shape[:along], *a.shape[along:]))
-        at += column.shape[along]
-    return tuple(done)
-
-
 def layer_norm(values, scale_gain):
     center = values - jnp.mean(values, axis=-1, keepdims=True)
     spread = jnp.mean(center * center, axis=-1, keepdims=True)
     return center * lax.rsqrt(spread + epsilon) * scale_gain.astype(jnp.float32)
 
 
-def depth_pass(gated_rows, segment, depth_kernel):
+def depth_pass(gated_rows, segment, kernel_rows):
     row_count = gated_rows.shape[0]
     margin = KERNEL // 2
     padded = jnp.pad(gated_rows, ((margin, margin), (0, 0)))
     labels = jnp.pad(segment, (margin, margin), constant_values=-1)
-    kernel_rows = depth_kernel.astype(jnp.float32)
     depthwise = jnp.zeros_like(gated_rows)
     for column in range(KERNEL):
         inside = (labels[column : column + row_count] == segment)[:, None]
@@ -48,21 +38,6 @@
             + jnp.where(inside, padded[column : column + row_count], 0.0) * kernel_rows[:, column]
         )
     return depthwise
-
-
-def conv_module(inputs, segment, params):
-    norm_gain, weight_in, depth_kernel, post_gain, weight_out = params
-    widths = inputs.shape[1]
-    source = inputs.astype(jnp.float32)
-    normed = layer_norm(source, norm_gain).astype(jnp.bfloat16)
-    projected = jnp.dot(normed, weight_in, preferred_element_type=jnp.float32)
-    gated_rows = projected[:, :widths] * jax.nn.sigmoid(projected[:, widths:])
-    depthwise = depth_pass(gated_rows, segment, depth_kernel)
-    normed_post = layer_norm(depthwise, post_gain)
-    active = (normed_post * jax.nn.sigmoid(normed_post)).astype(jnp.bfloat16)
-    return (source + jnp.dot(active, weight_out, preferred_element_type=jnp.float32)).astype(
-        jnp.bfloat16
-    )
 
 
 def relocate(own_part, next_part, prev_part):
@@ -84,10 +59,32 @@
 def shards(
     frames, lengths, destination, offsets, norm_gain, weight_in, depth_kernel, post_gain, weight_out
 ):
+    axes = ("dp", "group")
+    small = jnp.concatenate(
+        [norm_gain.reshape(-1, 1), post_gain.reshape(-1, 1), depth_kernel], axis=1
+    )
+    width = D // IN_CHUNKS
+    in_parts = []
+    for c in range(IN_CHUNKS):
+        columns = [
+            weight_in[:, c * width : (c + 1) * width],
+            weight_in[:, D + c * width : D + (c + 1) * width],
+        ]
+        if c == 0:
+            columns.append(small)
+        in_parts.append(lax.all_gather(jnp.concatenate(columns, axis=1), axes, axis=0, tiled=True))
+    small_all = in_parts[0][:, 2 * width :]
+    in_parts[0] = in_parts[0][:, : 2 * width]
+    out_width = D // OUT_CHUNKS
+    out_parts = [
+        lax.all_gather(weight_out[:, m * out_width : (m + 1) * out_width], axes, axis=0, tiled=True)
+        for m in range(OUT_CHUNKS)
+    ]
+    norm_full = small_all[:, 0]
+    post_full = small_all[:, 1]
+    kernel_full = small_all[:, 2:].astype(jnp.float32)
+
     dp_count = lax.axis_size("dp")
-    params = sent_together(
-        (norm_gain, weight_in, depth_kernel, post_gain, weight_out), ("dp", "group"), 0, 1
-    )
     my_index = lax.axis_index("dp")
     local_frames = frames[0]
     lengths_here = lengths[0]
@@ -118,8 +115,23 @@
         cut_utterance(local_frames, chosen[1]),
         cut_utterance(local_frames, chosen[2]),
     )
-    mixed = conv_module(received, segment, params)
-    return mixed[None]
+    source = received.astype(jnp.float32)
+    normed = layer_norm(source, norm_full).astype(jnp.bfloat16)
+    pieces = []
+    for c in range(IN_CHUNKS):
+        projected = jnp.dot(normed, in_parts[c], preferred_element_type=jnp.float32)
+        gated = projected[:, :width] * jax.nn.sigmoid(projected[:, width:])
+        pieces.append(depth_pass(gated, segment, kernel_full[c * width : (c + 1) * width]))
+    depthwise = jnp.concatenate(pieces, axis=1)
+    normed_post = layer_norm(depthwise, post_full)
+    active = (normed_post * jax.nn.sigmoid(normed_post)).astype(jnp.bfloat16)
+    outs = []
+    for m in range(OUT_CHUNKS):
+        mixed = source[:, m * out_width : (m + 1) * out_width] + jnp.dot(
+            active, out_parts[m], preferred_element_type=jnp.float32
+        )
+        outs.append(mixed.astype(jnp.bfloat16))
+    return jnp.concatenate(outs, axis=1)[None]
 
 
 def solution(mesh):

time: 225 us -> 730 us (3.24)
  waiting for transfers between devices: 84.5 us -> 563 us
  other arithmetic: 45.9 us -> 57.6 us
    all_gather x1 -> x6, waiting for transfers between devices: 84.5 us -> 563 us  [the longest x4 368 us: shards(): lax.all_gather(jnp.concatenate(columns, axis=1), axes, axis=0, tiled=True)]
    dot_general x2 -> x6, matrix products: 21.5 us -> 25.1 us  [the longest x4 14.3 us: shards(): projected = jnp.dot(normed, in_parts[c], preferred_element_type=jnp.float32)]
    reduce_sum x2 -> x5, other arithmetic: 20 us -> 23.1 us  [layer_norm(): center = values - jnp.mean(values, axis=-1, keepdims=True)]
    slice x2 -> x7, local copies, waits for them, and re-layouts: 17.5 us -> 20.4 us  [depth_pass(): kernel_rows[:, column]]
  transfers between devices with their start and end apart: 5 -> 10, of which waited for: 1 -> 6; matrix products, arithmetic and copies ran while one was open for 16% -> 15% of each run, Pallas kernels for 0% -> 0%
where the time goes in v1:
time: 730 us; the launch traced here: 725 us
  waiting for transfers between devices  563 us (77%)
  other arithmetic  57.6 us (8%)
  local copies, waits for them, and re-layouts  39.8 us (5%)
  between operations  29.5 us (4%)
  matrix products  25.1 us (3%)
  starting transfers between devices  9.56 us (1%)
    all_gather x4, waiting for transfers between devices, shards(): lax.all_gather(jnp.concatenate(columns, axis=1), axes, axis=0, tiled=True)  368 us
    all_gather x2, waiting for transfers between devices, shards(): lax.all_gather(weight_out[:, m * out_width:(m + 1) * out_width], axes, ax...  195 us
    reduce_sum x5, other arithmetic, layer_norm(): center = values - jnp.mean(values, axis=-1, keepdims=True)  23.1 us
    slice x7, local copies, waits for them, and re-layouts, depth_pass(): kernel_rows[:, column]  20.4 us
  transfers between devices with their start and end apart: 10, of which 6 were waited for; matrix products, arithmetic and copies ran while one was open for 15% of the time, Pallas kernels for 0%

profile of v1, /device:TPU:1, one launch (start us, length us, event | category | flops | bytes accessed | tf_op | source)
XLA Modules:
  0.0 724.6 jit_solution(8807620519260074038)
XLA Ops:
  6.5 0.8 fusion.216
  7.4 0.7 copy.12
  8.9 1.4 concatenate.18
  12.5 1.3 fusion.217
  13.9 0.8 reduce-window.9
  14.7 1.4 fusion.201
  16.1 3.3 select_reduce_fusion
  25.7 1.3 iota_compare_fusion.6
  27.0 3.5 bitcast_select_fusion
  30.6 2.7 collective-permute-start.1
  33.2 2.6 fusion.205
  35.8 2.6 pad_add_fusion
  39.1 6.0 collective-permute-start.2
  48.5 4.0 dynamic_update_slice.9
  56.2 1.9 select_select_fusion
  62.2 1.4 dynamic-slice_add_fusion.1
  63.6 4.0 dynamic_update_slice.10
  67.7 1.4 dynamic-slice_add_fusion
  69.1 4.6 dynamic_update_slice.11
  74.0 2.0 slice_convert_fusion
  76.6 54.1 %all-gather.7.cloned.1.call-done = bf16[2048,1058]{1,0:T(8,128)(2,1)} async-done(((bf16[8,1058]{1,0:T(8,128)(2,1)}), bf16[2048,1058]{1,0:T(8,128)(2,1)}) %all-gather.7.cloned.1.call-update) | async-done | bytes 4333584 | tf_op jit(solution)/shard_map/all_gather | solution.py:75
  130.7 1.2 slice_convert_fusion.1
  132.0 3.2 slice_reduce_fusion.122
  135.2 2.6 slice_reduce_fusion.126
  137.8 2.7 slice_reduce_fusion.125
  140.5 3.2 slice_reduce_fusion.124
  143.7 2.8 slice_reduce_fusion.127
  146.5 3.3 slice_reduce_fusion.123
  150.3 1.9 fusion
  152.2 2.6 slice_reduce_fusion.121
  154.8 1.1 fusion.19
  155.9 91.0 %all-gather.9.cloned.1.call-done = bf16[2048,1024]{1,0:T(8,128)(2,1)} async-done(((bf16[8,1024]{1,0:T(8,128)(2,1)}), bf16[2048,1024]{1,0:T(8,128)(2,1)}) %all-gather.9.cloned.1.call-update) | async-done | bytes 4194320 | tf_op jit(solution)/shard_map/all_gather | solution.py:75
  246.9 4.1 fusion.211
  250.9 1.1 fusion.15
  252.0 111.0 %all-gather.11.cloned.1.call-done = bf16[2048,1024]{1,0:T(8,128)(2,1)} async-done(((bf16[8,1024]{1,0:T(8,128)(2,1)}), bf16[2048,1024]{1,0:T(8,128)(2,1)}) %all-gather.11.cloned.1.call-update) | async-done | bytes 4194320 | tf_op jit(solution)/shard_map/all_gather | solution.py:75
  363.0 4.1 fusion.210
  367.3 111.7 %all-gather.13.cloned.1.call-done = bf16[2048,1024]{1,0:T(8,128)(2,1)} async-done(((bf16[8,1024]{1,0:T(8,128)(2,1)}), bf16[2048,1024]{1,0:T(8,128)(2,1)}) %all-gather.13.cloned.1.call-update) | async-done | bytes 4194320 | tf_op jit(solution)/shard_map/all_gather | solution.py:75
  479.1 4.3 fusion.209
  484.1 6.0 fusion.213
  490.3 6.1 fusion.212
  496.4 5.3 fusion.214
  501.8 5.3 fusion.215
  507.6 2.7 multiply_convert_fusion
  510.3 84.7 %all-gather.17.cloned.1.call-done = bf16[2048,1024]{1,0:T(8,128)(2,1)} async-done(((bf16[8,1024]{1,0:T(8,128)(2,1)}), bf16[2048,1024]{1,0:T(8,128)(2,1)}) %all-gather.17.cloned.1.call-update) | async-done | bytes 4194320 | tf_op jit(solution)/shard_map/all_gather | solution.py:80
  595.0 5.6 fusion.220
  600.6 110.4 %all-gather.15.cloned.1.call-done = bf16[2048,1024]{1,0:T(8,128)(2,1)} async-done(((bf16[8,1024]{1,0:T(8,128)(2,1)}), bf16[2048,1024]{1,0:T(8,128)(2,1)}) %all-gather.15.cloned.1.call-update) | async-done | bytes 4194320 | tf_op jit(solution)/shard_map/all_gather | solution.py:80
  711.0 5.2 fusion.3
  716.2 1.3 maximum_bitcast_fusion
  (133 shorter events, 8.7 us)
Async XLA Ops:
  6.5 26.7 %copy-start.43 = (s32[1,3]{1,0:T(1,128)S(1)}, s32[1,3]{1,0:T(1,128)}, u32[]{:S(2)}) copy-start(s32[1,3]{1,0:T(1,128)} %param.12) | copy-start | bytes 40
  6.5 124.2 %all-gather.7.cloned.1.call-start = ((), (), s32[]{:S(2)}) async-start(), calls=%async_computation | async-start | bytes 4737024 | tf_op jit(solution)/shard_map/all_gather | solution.py:75
  10.2 236.6 %all-gather.9.cloned.1.call-start = ((), (), s32[]{:S(2)}) async-start(), calls=%async_computation.1 | async-start | bytes 4210688 | tf_op jit(solution)/shard_map/all_gather | solution.py:75
  11.0 352.0 %all-gather.11.cloned.1.call-start = ((), (), s32[]{:S(2)}) async-start(), calls=%async_computation.2 | async-start | bytes 4210688 | tf_op jit(solution)/shard_map/all_gather | solution.py:75
  11.7 467.3 %all-gather.13.cloned.1.call-start = ((), (), s32[]{:S(2)}) async-start(), calls=%async_computation.3 | async-start | bytes 4210688 | tf_op jit(solution)/shard_map/all_gather | solution.py:75
  12.4 582.6 %all-gather.17.cloned.1.call-start = ((), (), s32[]{:S(2)}) async-start(), calls=%async_computation.5 | async-start | bytes 4210688 | tf_op jit(solution)/shard_map/all_gather | solution.py:80
  13.8 697.2 %all-gather.15.cloned.1.call-start = ((), (), s32[]{:S(2)}) async-start(), calls=%async_computation.4 | async-start | bytes 4210688 | tf_op jit(solution)/shard_map/all_gather | solution.py:80
  30.6 31.6 %collective-permute-start.1 = (bf16[192,2048]{1,0:T(8,128)(2,1)}, bf16[192,2048]{1,0:T(8,128)(2,1)}, u32[]{:S(2)}, u32[]{:S(2)}) collective-permute-start(bf16[192,2048]{1,0:T(8,128)(2,1)} %get-tuple-element.159), channel_id=1, source_target_pairs={{0,4},{4,8},{8,12},{12,16},{16,20},{20,24},{24,28},{28,32},{32,36}... | collective-permute-start | bytes 2359304 | tf_op jit(solution)/shard_map/ppermute | solution.py:19
  38.4 16.0 %collective-permute-start = (s32[2]{0:T(128)S(1)}, s32[2]{0:T(128)S(1)}, u32[]{:S(2)}, u32[]{:S(2)}) collective-permute-start(s32[2]{0:T(128)S(1)} %get-tuple-element.205), channel_id=1, source_target_pairs={{0,4},{4,8},{8,12},{12,16},{16,20},{20,24},{24,28},{28,32},{32,36}... | collective-permute-start | bytes 32 | tf_op jit(solution)/shard_map/ppermute | solution.py:19
  38.4 29.2 %collective-permute-start.3 = (bf16[192,2048]{1,0:T(8,128)(2,1)}, bf16[192,2048]{1,0:T(8,128)(2,1)}, u32[]{:S(2)}, u32[]{:S(2)}) collective-permute-start(bf16[192,2048]{1,0:T(8,128)(2,1)} %get-tuple-element.157), channel_id=1, source_target_pairs={{0,252},{4,0},{8,4},{12,8},{16,12},{20,16},{24,20},{28,24},{32,28}... | collective-permute-start | bytes 2359304 | tf_op jit(solution)/shard_map/ppermute | solution.py:19
  39.1 13.5 %collective-permute-start.2 = (s32[2]{0:T(128)S(1)}, s32[2]{0:T(128)S(1)}, u32[]{:S(2)}, u32[]{:S(2)}) collective-permute-start(s32[2]{0:T(128)S(1)} %get-tuple-element.206), channel_id=1, source_target_pairs={{0,252},{4,0},{8,4},{12,8},{16,12},{20,16},{24,20},{28,24},{32,28}... | collective-permute-start | bytes 32 | tf_op jit(solution)/shard_map/ppermute | solution.py:19
  76.0 287.0 %copy-start.41 = (f32[384]{0:T(512)}, f32[384]{0:T(512)S(1)}, u32[]{:S(2)}) copy-start(f32[384]{0:T(512)S(1)} %broadcast_multiply_fusion) | copy-start | bytes 4612
  76.6 286.4 %copy-start.42 = (f32[384]{0:T(512)}, f32[384]{0:T(512)S(1)}, u32[]{:S(2)}) copy-start(f32[384]{0:T(512)S(1)} %add_rsqrt_fusion.1) | copy-start | bytes 4612
  140.5 9.3 %slice-start = ((s8[4718592]{0:T(1024)(128)(4,1)}), s8[4194304]{0:T(1024)(128)(4,1)S(1)}, s32[]{:S(2)}) async-start(s8[4718592]{0:T(1024)(128)(4,1)} %bitcast.63), calls=%async_computation.6 | async-start | bytes 8388608
  143.7 6.1 slice-start.1
  479.0 4.9 copy-start.12
  479.0 4.9 copy-start.13
  479.0 4.9 copy-start.14
  479.1 4.9 copy-start.15
  479.1 4.9 copy-start.16
  479.1 4.9 copy-start.17
  479.1 4.9 copy-start.18
  479.1 4.9 copy-start.19
  479.1 4.9 copy-start.20
  483.4 6.7 copy-start.1
  483.4 6.7 copy-start.3
  483.5 6.7 copy-start.4
  483.5 6.7 copy-start.5
  483.5 6.7 copy-start.6
  483.5 6.7 copy-start.7
  483.5 6.7 copy-start.22
  483.5 6.7 copy-start.23
  483.5 6.7 copy-start.24
  483.5 6.7 copy-start.25
  483.5 6.7 copy-start.26
  483.5 6.7 copy-start.27
  483.6 6.7 copy-start.28
  483.6 6.7 copy-start.29
  483.6 6.7 copy-start.32
  483.6 6.7 copy-start.33
  483.6 6.7 copy-start.34
  483.6 6.7 copy-start.35
  483.6 6.7 copy-start.36
  483.6 6.7 copy-start.37
  483.6 6.7 copy-start.38
  483.6 6.7 copy-start.39
  483.7 6.7 copy-start.40
  510.3 200.7 %copy-start = (f32[384,2048]{1,0:T(8,128)S(1)}, f32[384,2048]{1,0:T(8,128)}, u32[]{:S(2)}) copy-start(f32[384,2048]{1,0:T(8,128)} %slice_convert_fusion) | copy-start | bytes 9437188
  (8 other events, 39.3 us)
Sparse Core Ops, SparseCore 0:
  11.1 119.5 all-gather.6
  134.4 112.3 all-gather.8
  250.6 112.3 all-gather.10
  366.6 112.3 all-gather.12
  482.6 112.3 all-gather.16
  598.6 112.3 all-gather.14

commit v2 on v0

--- a/solution.py
+++ b/solution.py
@@ -1,6 +1,8 @@
 import jax
 import jax.numpy as jnp
 from jax import lax
+from jax.experimental import pallas as pl
+from jax.experimental.pallas import tpu as pltpu
 from jax.sharding import PartitionSpec as P
 
 D = 2048
@@ -34,32 +36,69 @@
     return center * lax.rsqrt(spread + epsilon) * scale_gain.astype(jnp.float32)
 
 
-def depth_pass(gated_rows, segment, depth_kernel):
-    row_count = gated_rows.shape[0]
+ROW_CHUNK = 128
+LANE_BLOCK = 128
+
+
+def depth_kernel_body(padded_ref, labels_ref, taps_ref, gain_ref, out_ref, mask_ref, acc_ref):
+    rows = out_ref.shape[0]
+    margin = KERNEL // 2
+    for column in range(KERNEL):
+        same = labels_ref[column : column + rows, :] == labels_ref[margin : margin + rows, :]
+        mask_ref[column] = jnp.where(same, 1.0, 0.0)
+
+    def lane_block(index, carry):
+        lanes = pl.ds(pl.multiple_of(index * LANE_BLOCK, LANE_BLOCK), LANE_BLOCK)
+        for chunk in range(rows // ROW_CHUNK):
+            low = chunk * ROW_CHUNK
+            total = jnp.zeros((ROW_CHUNK, LANE_BLOCK), jnp.float32)
+            for column in range(KERNEL):
+                shifted = padded_ref[low + column : low + column + ROW_CHUNK, lanes]
+                weight = mask_ref[column, low : low + ROW_CHUNK, :]
+                total = total + shifted * weight * taps_ref[column : column + 1, lanes]
+            acc_ref[low : low + ROW_CHUNK, lanes] = total
+        return carry
+
+    lax.fori_loop(0, out_ref.shape[1] // LANE_BLOCK, lane_block, 0)
+    for chunk in range(rows // ROW_CHUNK):
+        low = chunk * ROW_CHUNK
+        values = acc_ref[low : low + ROW_CHUNK, :]
+        center = values - jnp.mean(values, axis=-1, keepdims=True)
+        spread = jnp.mean(center * center, axis=-1, keepdims=True)
+        normed = center * lax.rsqrt(spread + epsilon) * gain_ref[...]
+        out_ref[low : low + ROW_CHUNK, :] = (normed * jax.nn.sigmoid(normed)).astype(out_ref.dtype)
+
+
+def depth_and_norm(gated_rows, segment, taps, post_gain):
+    rows, width = gated_rows.shape
     margin = KERNEL // 2
     padded = jnp.pad(gated_rows, ((margin, margin), (0, 0)))
     labels = jnp.pad(segment, (margin, margin), constant_values=-1)
-    kernel_rows = depth_kernel.astype(jnp.float32)
-    depthwise = jnp.zeros_like(gated_rows)
-    for column in range(KERNEL):
-        inside = (labels[column : column + row_count] == segment)[:, None]
-        depthwise = (
-            depthwise
-            + jnp.where(inside, padded[column : column + row_count], 0.0) * kernel_rows[:, column]
-        )
-    return depthwise
+    labels = jnp.broadcast_to(labels[:, None], (rows + 2 * margin, LANE_BLOCK))
+    return pl.pallas_call(
+        depth_kernel_body,
+        out_shape=jax.ShapeDtypeStruct((rows, width), jnp.bfloat16),
+        in_specs=[pl.BlockSpec(memory_space=pltpu.VMEM)] * 4,
+        out_specs=pl.BlockSpec(memory_space=pltpu.VMEM),
+        scratch_shapes=[
+            pltpu.VMEM((KERNEL, rows, LANE_BLOCK), jnp.float32),
+            pltpu.VMEM((rows, width), jnp.float32),
+        ],
+        compiler_params=pltpu.CompilerParams(vmem_limit_bytes=48 * 1024 * 1024),
+        cost_estimate=pl.CostEstimate(
+            flops=3 * KERNEL * rows * width, transcendentals=rows * width, bytes_accessed=6 * rows * width
+        ),
+    )(padded, labels, taps, post_gain)
 
 
 def conv_module(inputs, segment, params):
-    norm_gain, weight_in, depth_kernel, post_gain, weight_out = params
+    norm_gain, weight_in, taps, post_gain, weight_out = params
     widths = inputs.shape[1]
     source = inputs.astype(jnp.float32)
     normed = layer_norm(source, norm_gain).astype(jnp.bfloat16)
     projected = jnp.dot(normed, weight_in, preferred_element_type=jnp.float32)
     gated_rows = projected[:, :widths] * jax.nn.sigmoid(projected[:, widths:])
-    depthwise = depth_pass(gated_rows, segment, depth_kernel)
-    normed_post = layer_norm(depthwise, post_gain)
-    active = (normed_post * jax.nn.sigmoid(normed_post)).astype(jnp.bfloat16)
+    active = depth_and_norm(gated_rows, segment, taps, post_gain)
     return (source + jnp.dot(active, weight_out, preferred_element_type=jnp.float32)).astype(
         jnp.bfloat16
     )
@@ -85,8 +124,17 @@
     frames, lengths, destination, offsets, norm_gain, weight_in, depth_kernel, post_gain, weight_out
 ):
     dp_count = lax.axis_size("dp")
-    params = sent_together(
-        (norm_gain, weight_in, depth_kernel, post_gain, weight_out), ("dp", "group"), 0, 1
+    small = jnp.concatenate([norm_gain[:, None], post_gain[:, None], depth_kernel], axis=1)
+    both = jnp.concatenate([weight_in, weight_out, small], axis=1)
+    gathered = lax.all_gather(both, ("dp", "group"), axis=0, tiled=True)
+    columns = weight_in.shape[1] + weight_out.shape[1]
+    small_t = jnp.transpose(gathered[:, columns:]).astype(jnp.float32)
+    params = (
+        small_t[0:1],
+        gathered[:, : weight_in.shape[1]],
+        small_t[2:],
+        small_t[1:2],
+        gathered[:, weight_in.shape[1] : columns],
     )
     my_index = lax.axis_index("dp")
     local_frames = frames[0]

time: 225 us -> 210 us (0.933)
  Pallas kernels: 0 us -> 27.1 us
  other arithmetic: 45.9 us -> 22.4 us
  local copies, waits for them, and re-layouts: 34.4 us -> 18.7 us
  matrix products: 21.5 us -> 18.3 us
    pallas_call x0 -> x1, Pallas kernels: none -> 27.1 us  [depth_and_norm(): pl.pallas_call(depth_kernel_body, out_shape=jax.ShapeDtypeStruct((rows, w...]
    reduce_sum x2 -> x1, other arithmetic: 20 us -> 0.29 us  [layer_norm(): center = values - jnp.mean(values, axis=-1, keepdims=True)]
    slice x2 -> x3, local copies, waits for them, and re-layouts: 17.5 us -> 1.11 us  [the longest x1 1.08 us: shards(): small_t = jnp.transpose(gathered[:, columns:]).astype(jnp.float32)]
    convert_element_type x2 -> x1, other arithmetic: 2.99 us -> 0.02 us  [shards(): small_t = jnp.transpose(gathered[:, columns:]).astype(jnp.float32)]
  transfers between devices with their start and end apart: 5 -> 5, of which waited for: 1 -> 1; matrix products, arithmetic and copies ran while one was open for 16% -> 17% of each run, Pallas kernels for 0% -> 0%
where the time goes in v2:
time: 210 us
  waiting for transfers between devices  85.3 us (41%)
  between operations  28.5 us (14%)
  Pallas kernels  27.1 us (13%)
  other arithmetic  22.4 us (11%)
  local copies, waits for them, and re-layouts  18.7 us (9%)
  matrix products  18.3 us (9%)
  starting transfers between devices  9.36 us (4%)
    all_gather x1, waiting for transfers between devices, shards(): gathered = lax.all_gather(both, ('dp', 'group'), axis=0, tiled=True)  85.3 us
    pallas_call x1, Pallas kernels, depth_and_norm(): pl.pallas_call(depth_kernel_body, out_shape=jax.ShapeDtypeStruct((rows, w...  27.1 us
    dynamic_update_slice x3, local copies, waits for them, and re-layouts, relocate(): lax.dynamic_update_slice_in_dim(received, current + frame_rows, meta_data...  12.1 us
    dot_general x1, matrix products, conv_module(): projected = jnp.dot(normed, weight_in, preferred_element_type=jnp.float32)  10.4 us
    ppermute x4, starting transfers between devices, shifted(): lax.ppermute(array, axis, [(i, (i + by) % peers) for i in range(peers)])  9.36 us
    dot_general x1, matrix products, conv_module(): jnp.dot(active, weight_out, preferred_element_type=jnp.float32)  7.95 us
    reduce_sum x2, other arithmetic, pick_entry(): return jnp.sum(jnp.where(slot_ids == which, values, 0))  5.76 us
  transfers between devices with their start and end apart: 5, of which 1 were waited for; matrix products, arithmetic and copies ran while one was open for 17% of the time, Pallas kernels for 0%

profile of v2, /device:TPU:1, one launch (start us, length us, event | category | flops | bytes accessed | tf_op | source)
XLA Modules:
  0.0 209.7 jit_solution(1094422782455522726)
XLA Ops:
  6.5 0.0 copy-start
  6.5 0.0 all-gather.2.cloned.1.call-start
  6.5 0.8 copy.13
  7.3 0.7 copy.14
  8.0 1.6 concatenate.3
  9.6 0.0 all-gather.2.cloned.1.call-update
  9.6 0.8 reduce-window.9
  10.5 1.4 fusion.29
  11.8 3.2 %select_reduce_fusion = (s32[]{:T(128)}, s32[]{:T(128)}, s32[]{:T(128)}, s32[]{:T(128)}, s32[]{:T(128)}, /*index=5*/s32[]{:T(128)}) fusion(s32[]{:T(128)} %get-tuple-element.14, s32[1,3]{1,0:T(1,128)} %param.10, s32[3,1]{0,1:T(1,128)S(1)} %reduce-window.9, s32[]{:T(128)} %get-tuple-element.15, s32[]{:T(128)} %get-tuple-element.16), kind=kLoop, calls=%fused_computation.69 | loop fusion | flops 42 | bytes 60 | tf_op jit(solution)/shard_map/reduce_sum | solution.py:149
  20.6 0.6 iota_compare_fusion.8
  21.2 1.2 iota_compare_fusion.6
  22.4 3.5 %bitcast_select_fusion = (bf16[192,2048]{1,0:T(8,128)(2,1)}, bf16[192,2048]{1,0:T(8,128)(2,1)S(1)}, bf16[192,2048]{1,0:T(8,128)(2,1)}) fusion(bf16[1,576,2048]{2,1,0:T(8,128)(2,1)} %param.9, s32[]{:T(128)S(6)} %select_n.104, pred[192]{0:T(512)(128)(4,1)S(1)} %get-tuple-element.28, s32[]{:T(128)S(6)} %select_n.88, pred[192]{0:T(512)(128)(4,1)S(1)} %iota_compare_fusion.8, ...), kind=kLoop, calls=%fused_computation.23 | loop fusion | flops 1179648 | bytes 4719180 | tf_op jit(solution)/shard_map/jit(_where)/select_n | solution.py:161
  26.0 2.7 %collective-permute-start.1 = (bf16[192,2048]{1,0:T(8,128)(2,1)}, bf16[192,2048]{1,0:T(8,128)(2,1)}, u32[]{:S(2)}, u32[]{:S(2)}) collective-permute-start(bf16[192,2048]{1,0:T(8,128)(2,1)} %get-tuple-element.19), channel_id=1, source_target_pairs={{0,4},{4,8},{8,12},{12,16},{16,20},{20,24},{24,28},{28,32},{32,36}... | collective-permute-start | bytes 2359304 | tf_op jit(solution)/shard_map/ppermute | solution.py:19
  28.7 0.0 copy-done
  28.7 2.5 %fusion.33 = (s32[]{:T(128)}, s32[]{:T(128)}, s32[]{:T(128)}) fusion(s32[1,3]{1,0:T(1,128)S(1)} %copy-done, s32[]{:T(128)} %get-tuple-element.14, s32[]{:T(128)} %get-tuple-element.15, s32[]{:T(128)} %get-tuple-element.16), kind=kLoop, calls=%fused_computation.61 | loop fusion | flops 24 | bytes 36 | tf_op jit(solution)/shard_map/reduce_sum | solution.py:149
  31.2 2.5 %pad_add_fusion = (s32[2]{0:T(128)S(1)}, s32[2]{0:T(128)S(1)}) fusion(s32[1]{0:T(128)} %bitcast.7, s32[1]{0:T(128)} %bitcast.6, s32[1]{0:T(128)} %bitcast.11, s32[1]{0:T(128)} %bitcast.10), kind=kLoop, calls=%fused_computation.54 | loop fusion | flops 4 | bytes 32 | tf_op jit(solution)/shard_map/stack | solution.py:162
  33.7 0.0 collective-permute-start
  33.7 0.6 collective-permute-start.3
  34.3 6.0 %collective-permute-start.2 = (s32[2]{0:T(128)S(1)}, s32[2]{0:T(128)S(1)}, u32[]{:S(2)}, u32[]{:S(2)}) collective-permute-start(s32[2]{0:T(128)S(1)} %get-tuple-element.27), channel_id=1, source_target_pairs={{0,252},{4,0},{8,4},{12,8},{16,12},{20,16},{24,20},{28,24},{32,28}... | collective-permute-start | bytes 32 | tf_op jit(solution)/shard_map/ppermute | solution.py:19
  43.5 0.3 broadcast_in_dim.67
  43.7 4.0 %dynamic_update_slice.9 = bf16[576,2048]{1,0:T(8,128)(2,1)S(1)} dynamic-update-slice(bf16[576,2048]{1,0:T(8,128)(2,1)S(1)} %broadcast_in_dim.67, bf16[192,2048]{1,0:T(8,128)(2,1)S(1)} %get-tuple-element.18, s32[]{:T(128)S(6)} %select_n.91, s32[]{:T(128)} %constant.22.clone.1) | dynamic-update-slice | bytes 1572868 | tf_op jit(solution)/shard_map/dynamic_update_slice | solution.py:117
  47.8 0.0 collective-permute-done
  47.8 0.6 fusion.39
  49.6 0.0 collective-permute-done.2
  49.7 0.6 fusion.38
  55.3 1.8 select_select_fusion
  57.2 0.1 pad.9
  57.3 0.0 collective-permute-done.1
  57.3 1.4 dynamic-slice_add_fusion.1
  58.7 4.0 %dynamic_update_slice.10 = bf16[576,2048]{1,0:T(8,128)(2,1)S(1)} dynamic-update-slice(bf16[576,2048]{1,0:T(8,128)(2,1)S(1)} %dynamic_update_slice.9, bf16[192,2048]{1,0:T(8,128)(2,1)S(1)} %dynamic-slice_add_fusion.1, s32[]{:T(128)S(6)} %select_n.95, s32[]{:T(128)} %constant.22.clone.1) | dynamic-update-slice | bytes 1572868 | tf_op jit(solution)/shard_map/dynamic_update_slice | solution.py:117
  62.8 0.0 collective-permute-done.3
  62.8 1.4 dynamic-slice_add_fusion
  64.2 4.0 %dynamic_update_slice.11 = bf16[576,2048]{1,0:T(8,128)(2,1)S(1)} dynamic-update-slice(bf16[576,2048]{1,0:T(8,128)(2,1)S(1)} %dynamic_update_slice.10, bf16[192,2048]{1,0:T(8,128)(2,1)S(1)} %dynamic-slice_add_fusion, s32[]{:T(128)S(6)} %select_n.102, s32[]{:T(128)} %constant.22.clone.1) | dynamic-update-slice | bytes 1572868 | tf_op jit(solution)/shard_map/dynamic_update_slice | solution.py:117
  68.3 0.3 convert_reduce_fusion
  68.6 0.6 fusion.6
  69.1 85.3 %all-gather.2.cloned.1.call-done = bf16[2048,6178]{1,0:T(8,128)(2,1)} async-done(((bf16[8,6178]{1,0:T(8,128)(2,1)}), bf16[2048,6178]{1,0:T(8,128)(2,1)}) %all-gather.2.cloned.1.call-update) | async-done | bytes 25305104 | tf_op jit(solution)/shard_map/all_gather | solution.py:129
  154.4 1.1 slice.59
  155.5 0.2 copy.16
  155.8 10.4 %fusion = f32[384,4096]{1,0:T(8,128)S(1)} fusion(bf16[2048,6178]{1,0:T(8,128)(2,1)} %all-gather.2.cloned.1.call-done, f32[2048]{0:T(1024)S(1)} %bitcast.60, f32[384]{0:T(512)S(1)} %add_rsqrt_fusion, f32[384]{0:T(512)S(1)} %broadcast_multiply_fusion, bf16[576,2048]{1,0:T(8,128)(2,1)S(1)} %dynamic_update_slice.11), kind=kOutput, calls=%fused_computation | convolution fusion | flops 6446383104 | bytes 24653824 | tf_op jit(solution)/shard_map/dot_general | solution.py:99
  166.2 1.0 fusion.13
  167.2 0.5 pad.8.padded_ref
  167.7 0.1 broadcast_in_dim.77.labels_ref
  167.8 27.1 %shard_map.91 = bf16[384,2048]{1,0:T(8,128)(2,1)S(1)} custom-call(f32[416,2048]{1,0:T(8,128)S(1)} %pad.8.padded_ref, s32[416,128]{1,0:T(8,128)S(1)} %broadcast_in_dim.77.labels_ref, f32[32,2048]{1,0:T(8,128)S(1)} %slice.64.taps_ref, f32[1,2048]{1,0:T(1,128)S(1)} %get-tuple-element.20.gain_ref), custom_call_target="tpu_custom_call" | custom-call | flops 75497472 | bytes 4718592 | tf_op jit(solution)/shard_map/pallas_call | solution.py:78
  194.9 8.0 %fusion.16 = bf16[1,384,2048]{2,1,0:T(8,128)(2,1)} fusion(bf16[384,2048]{1,0:T(8,128)(2,1)S(1)} %shard_map.91, bf16[2048,6178]{1,0:T(8,128)(2,1)} %all-gather.2.cloned.1.call-done, bf16[576,2048]{1,0:T(8,128)(2,1)S(1)} %dynamic_update_slice.11), kind=kOutput, calls=%fused_computation.18 | convolution fusion | flops 3223584768 | bytes 13107200 | tf_op jit(solution)/shard_map/dot_general | solution.py:102
  (5 shorter events, 0.1 us)
Async XLA Ops:
  6.5 22.1 %copy-start = (s32[1,3]{1,0:T(1,128)S(1)}, s32[1,3]{1,0:T(1,128)}, u32[]{:S(2)}) copy-start(s32[1,3]{1,0:T(1,128)} %param.12) | copy-start | bytes 40
  6.5 147.9 %all-gather.2.cloned.1.call-start = ((), (), s32[]{:S(2)}) async-start(), calls=%async_computation | async-start | bytes 25790464 | tf_op jit(solution)/shard_map/all_gather | solution.py:129
  26.0 31.3 %collective-permute-start.1 = (bf16[192,2048]{1,0:T(8,128)(2,1)}, bf16[192,2048]{1,0:T(8,128)(2,1)}, u32[]{:S(2)}, u32[]{:S(2)}) collective-permute-start(bf16[192,2048]{1,0:T(8,128)(2,1)} %get-tuple-element.19), channel_id=1, source_target_pairs={{0,4},{4,8},{8,12},{12,16},{16,20},{20,24},{24,28},{28,32},{32,36}... | collective-permute-start | bytes 2359304 | tf_op jit(solution)/shard_map/ppermute | solution.py:19
  33.7 14.1 %collective-permute-start = (s32[2]{0:T(128)S(1)}, s32[2]{0:T(128)S(1)}, u32[]{:S(2)}, u32[]{:S(2)}) collective-permute-start(s32[2]{0:T(128)S(1)} %get-tuple-element.26), channel_id=1, source_target_pairs={{0,4},{4,8},{8,12},{12,16},{16,20},{20,24},{24,28},{28,32},{32,36}... | collective-permute-start | bytes 32 | tf_op jit(solution)/shard_map/ppermute | solution.py:19
  33.7 29.0 %collective-permute-start.3 = (bf16[192,2048]{1,0:T(8,128)(2,1)}, bf16[192,2048]{1,0:T(8,128)(2,1)}, u32[]{:S(2)}, u32[]{:S(2)}) collective-permute-start(bf16[192,2048]{1,0:T(8,128)(2,1)} %get-tuple-element.17), channel_id=1, source_target_pairs={{0,252},{4,0},{8,4},{12,8},{16,12},{20,16},{24,20},{28,24},{32,28}... | collective-permute-start | bytes 2359304 | tf_op jit(solution)/shard_map/ppermute | solution.py:19
  34.3 15.3 %collective-permute-start.2 = (s32[2]{0:T(128)S(1)}, s32[2]{0:T(128)S(1)}, u32[]{:S(2)}, u32[]{:S(2)}) collective-permute-start(s32[2]{0:T(128)S(1)} %get-tuple-element.27), channel_id=1, source_target_pairs={{0,252},{4,0},{8,4},{12,8},{16,12},{20,16},{24,20},{28,24},{32,28}... | collective-permute-start | bytes 32 | tf_op jit(solution)/shard_map/ppermute | solution.py:19
Sparse Core Ops, SparseCore 0:
  11.1 143.2 all-gather.1

commit v3 on v2

--- a/solution.py
+++ b/solution.py
@@ -38,67 +38,96 @@
 
 ROW_CHUNK = 128
 LANE_BLOCK = 128
-
-
-def depth_kernel_body(padded_ref, labels_ref, taps_ref, gain_ref, out_ref, mask_ref, acc_ref):
+BLOCK = 256
+
+
+def fused_body(normed_ref, value_ref, gate_ref, labels_ref, taps_ref, gain_ref, out_ref, gated_ref, mask_ref, acc_ref):
+    step = pl.program_id(0)
+    blocks = pl.num_programs(0) - 1
     rows = out_ref.shape[0]
     margin = KERNEL // 2
-    for column in range(KERNEL):
-        same = labels_ref[column : column + rows, :] == labels_ref[margin : margin + rows, :]
-        mask_ref[column] = jnp.where(same, 1.0, 0.0)
-
-    def lane_block(index, carry):
-        lanes = pl.ds(pl.multiple_of(index * LANE_BLOCK, LANE_BLOCK), LANE_BLOCK)
+
+    @pl.when(step == 0)
+    def _():
+        for column in range(KERNEL):
+            same = labels_ref[column : column + rows, :] == labels_ref[margin : margin + rows, :]
+            mask_ref[column] = jnp.where(same, 1.0, 0.0)
+        gated_ref[...] = jnp.zeros(gated_ref.shape, jnp.float32)
+
+    normed = normed_ref[...]
+    projected = jnp.dot(normed, value_ref[...], preferred_element_type=jnp.float32)
+    gates = jnp.dot(normed, gate_ref[...], preferred_element_type=jnp.float32)
+    gated_ref[step % 2, margin : margin + rows, :] = projected * jax.nn.sigmoid(gates)
+
+    done = jnp.maximum(step - 1, 0)
+    slot = (step + 1) % 2
+    for half in range(BLOCK // LANE_BLOCK):
+        lanes = pl.ds(pl.multiple_of(done * BLOCK + half * LANE_BLOCK, LANE_BLOCK), LANE_BLOCK)
+        inner = slice(half * LANE_BLOCK, (half + 1) * LANE_BLOCK)
         for chunk in range(rows // ROW_CHUNK):
             low = chunk * ROW_CHUNK
             total = jnp.zeros((ROW_CHUNK, LANE_BLOCK), jnp.float32)
             for column in range(KERNEL):
-                shifted = padded_ref[low + column : low + column + ROW_CHUNK, lanes]
+                shifted = gated_ref[slot, low + column : low + column + ROW_CHUNK, inner]
                 weight = mask_ref[column, low : low + ROW_CHUNK, :]
                 total = total + shifted * weight * taps_ref[column : column + 1, lanes]
             acc_ref[low : low + ROW_CHUNK, lanes] = total
-        return carry
-
-    lax.fori_loop(0, out_ref.shape[1] // LANE_BLOCK, lane_block, 0)
-    for chunk in range(rows // ROW_CHUNK):
-        low = chunk * ROW_CHUNK
-        values = acc_ref[low : low + ROW_CHUNK, :]
-        center = values - jnp.mean(values, axis=-1, keepdims=True)
-        spread = jnp.mean(center * center, axis=-1, keepdims=True)
-        normed = center * lax.rsqrt(spread + epsilon) * gain_ref[...]
-        out_ref[low : low + ROW_CHUNK, :] = (normed * jax.nn.sigmoid(normed)).astype(out_ref.dtype)
-
-
-def depth_and_norm(gated_rows, segment, taps, post_gain):
-    rows, width = gated_rows.shape
+
+    @pl.when(step == blocks)
+    def _():
+        for chunk in range(rows // ROW_CHUNK):
+            low = chunk * ROW_CHUNK
+            values = acc_ref[low : low + ROW_CHUNK, :]
+            center = values - jnp.mean(values, axis=-1, keepdims=True)
+            spread = jnp.mean(center * center, axis=-1, keepdims=True)
+            normed_post = center * lax.rsqrt(spread + epsilon) * gain_ref[...]
+            out_ref[low : low + ROW_CHUNK, :] = (
+                normed_post * jax.nn.sigmoid(normed_post)
+            ).astype(out_ref.dtype)
+
+
+def fused_projection(normed, gathered, segment, taps, post_gain):
+    rows, width = normed.shape
     margin = KERNEL // 2
-    padded = jnp.pad(gated_rows, ((margin, margin), (0, 0)))
+    blocks = width // BLOCK
     labels = jnp.pad(segment, (margin, margin), constant_values=-1)
     labels = jnp.broadcast_to(labels[:, None], (rows + 2 * margin, LANE_BLOCK))
+    last = blocks - 1
+    whole = lambda s: (0, 0)
     return pl.pallas_call(
-        depth_kernel_body,
+        fused_body,
+        grid=(blocks + 1,),
         out_shape=jax.ShapeDtypeStruct((rows, width), jnp.bfloat16),
-        in_specs=[pl.BlockSpec(memory_space=pltpu.VMEM)] * 4,
-        out_specs=pl.BlockSpec(memory_space=pltpu.VMEM),
+        in_specs=[
+            pl.BlockSpec((rows, width), whole),
+            pl.BlockSpec((width, BLOCK), lambda s: (0, jnp.minimum(s, last))),
+            pl.BlockSpec((width, BLOCK), lambda s: (0, blocks + jnp.minimum(s, last))),
+            pl.BlockSpec((rows + 2 * margin, LANE_BLOCK), whole),
+            pl.BlockSpec((KERNEL, width), whole),
+            pl.BlockSpec((1, width), whole),
+        ],
+        out_specs=pl.BlockSpec((rows, width), whole),
         scratch_shapes=[
+            pltpu.VMEM((2, rows + 2 * margin, BLOCK), jnp.float32),
             pltpu.VMEM((KERNEL, rows, LANE_BLOCK), jnp.float32),
             pltpu.VMEM((rows, width), jnp.float32),
         ],
-        compiler_params=pltpu.CompilerParams(vmem_limit_bytes=48 * 1024 * 1024),
+        compiler_params=pltpu.CompilerParams(
+            dimension_semantics=("arbitrary",), vmem_limit_bytes=56 * 1024 * 1024
+        ),
         cost_estimate=pl.CostEstimate(
-            flops=3 * KERNEL * rows * width, transcendentals=rows * width, bytes_accessed=6 * rows * width
+            flops=2 * rows * width * 2 * width + 3 * KERNEL * rows * width,
+            transcendentals=2 * rows * width,
+            bytes_accessed=2 * width * 2 * width + 8 * rows * width,
         ),
-    )(padded, labels, taps, post_gain)
+    )(normed, gathered, gathered, labels, taps, post_gain)
 
 
 def conv_module(inputs, segment, params):
-    norm_gain, weight_in, taps, post_gain, weight_out = params
-    widths = inputs.shape[1]
+    norm_gain, gathered, taps, post_gain, weight_out = params
     source = inputs.astype(jnp.float32)
     normed = layer_norm(source, norm_gain).astype(jnp.bfloat16)
-    projected = jnp.dot(normed, weight_in, preferred_element_type=jnp.float32)
-    gated_rows = projected[:, :widths] * jax.nn.sigmoid(projected[:, widths:])
-    active = depth_and_norm(gated_rows, segment, taps, post_gain)
+    active = fused_projection(normed, gathered, segment, taps, post_gain)
     return (source + jnp.dot(active, weight_out, preferred_element_type=jnp.float32)).astype(
         jnp.bfloat16
     )
@@ -131,7 +160,7 @@
     small_t = jnp.transpose(gathered[:, columns:]).astype(jnp.float32)
     params = (
         small_t[0:1],
-        gathered[:, : weight_in.shape[1]],
+        gathered,
         small_t[2:],
         small_t[1:2],
         gathered[:, weight_in.shape[1] : columns],

time: 210 us -> 215 us (1.024)
  Pallas kernels: 27.1 us -> 39 us
  matrix products: 18.3 us -> 8.42 us
    pallas_call x1, Pallas kernels: 27.1 us -> 39 us  [fused_projection(): pl.pallas_call(fused_body, grid=(blocks + 1,), out_shape=jax.ShapeDtypeSt...]
    dot_general x1 -> x0, matrix products: 10.4 us -> none  [conv_module(): projected = jnp.dot(normed, weight_in, preferred_element_type=jnp.float32)]
  transfers between devices with their start and end apart: 5 -> 5, of which waited for: 1 -> 1; matrix products, arithmetic and copies ran while one was open for 17% -> 16% of each run, Pallas kernels for 0% -> 0%
where the time goes in v3:
time: 215 us; the launch traced here: 214 us
  waiting for transfers between devices  85.3 us (40%)
  Pallas kernels  39 us (18%)
  between operations  28.4 us (13%)
  other arithmetic  23.1 us (11%)
  local copies, waits for them, and re-layouts  20.3 us (9%)
  starting transfers between devices  9.34 us (4%)
  matrix products  8.42 us (4%)
    all_gather x1, waiting for transfers between devices, shards(): gathered = lax.all_gather(both, ('dp', 'group'), axis=0, tiled=True)  85.3 us
    pallas_call x1, Pallas kernels, fused_projection(): pl.pallas_call(fused_body, grid=(blocks + 1,), out_shape=jax.ShapeDtypeSt...  39 us
    dynamic_update_slice x3, local copies, waits for them, and re-layouts, relocate(): lax.dynamic_update_slice_in_dim(received, current + frame_rows, meta_data...  12.1 us
    ppermute x4, starting transfers between devices, shifted(): lax.ppermute(array, axis, [(i, (i + by) % peers) for i in range(peers)])  9.34 us
    dot_general x1, matrix products, conv_module(): jnp.dot(active, weight_out, preferred_element_type=jnp.float32)  8.42 us
    reduce_sum x2, other arithmetic, pick_entry(): return jnp.sum(jnp.where(slot_ids == which, values, 0))  5.76 us
  transfers between devices with their start and end apart: 5, of which 1 were waited for; matrix products, arithmetic and copies ran while one was open for 16% of the time, Pallas kernels for 0%

profile of v3, /device:TPU:1, one launch (start us, length us, event | category | flops | bytes accessed | tf_op | source)
XLA Modules:
  0.0 213.9 jit_solution(16672170363268111719)
XLA Ops:
  6.5 0.0 all-gather.2.cloned.1.call-start
  6.5 0.7 copy.15
  7.3 0.7 copy.16
  8.0 1.6 concatenate.3
  9.6 0.0 all-gather.2.cloned.1.call-update
  9.6 0.8 reduce-window.9
  10.4 1.4 fusion.18
  11.8 3.2 %select_reduce_fusion = (s32[]{:T(128)}, s32[]{:T(128)}, s32[]{:T(128)}, s32[]{:T(128)}, s32[]{:T(128)}, /*index=5*/s32[]{:T(128)}) fusion(s32[]{:T(128)} %get-tuple-element.14, s32[1,3]{1,0:T(1,128)} %param.10, s32[3,1]{0,1:T(1,128)S(1)} %reduce-window.9, s32[]{:T(128)} %get-tuple-element.15, s32[]{:T(128)} %get-tuple-element.16), kind=kLoop, calls=%fused_computation.58 | loop fusion | flops 42 | bytes 60 | tf_op jit(solution)/shard_map/reduce_sum | solution.py:178
  20.6 0.6 iota_compare_fusion.8
  21.2 1.2 iota_compare_fusion.6
  22.4 0.0 copy-start
  22.4 3.5 %bitcast_select_fusion = (bf16[192,2048]{1,0:T(8,128)(2,1)}, bf16[192,2048]{1,0:T(8,128)(2,1)S(1)}, bf16[192,2048]{1,0:T(8,128)(2,1)}) fusion(bf16[1,576,2048]{2,1,0:T(8,128)(2,1)} %param.9, s32[]{:T(128)S(6)} %select_n.104, pred[192]{0:T(512)(128)(4,1)S(1)} %get-tuple-element.28, s32[]{:T(128)S(6)} %select_n.88, pred[192]{0:T(512)(128)(4,1)S(1)} %iota_compare_fusion.8, ...), kind=kLoop, calls=%fused_computation.12 | loop fusion | flops 1179648 | bytes 4719180 | tf_op jit(solution)/shard_map/jit(_where)/select_n | solution.py:190
  26.0 2.7 %collective-permute-start.1 = (bf16[192,2048]{1,0:T(8,128)(2,1)}, bf16[192,2048]{1,0:T(8,128)(2,1)}, u32[]{:S(2)}, u32[]{:S(2)}) collective-permute-start(bf16[192,2048]{1,0:T(8,128)(2,1)} %get-tuple-element.19), channel_id=1, source_target_pairs={{0,4},{4,8},{8,12},{12,16},{16,20},{20,24},{24,28},{28,32},{32,36}... | collective-permute-start | bytes 2359304 | tf_op jit(solution)/shard_map/ppermute | solution.py:19
  28.6 0.0 copy-done
  28.6 2.5 %fusion.22 = (s32[]{:T(128)}, s32[]{:T(128)}, s32[]{:T(128)}) fusion(s32[1,3]{1,0:T(1,128)S(1)} %copy-done, s32[]{:T(128)} %get-tuple-element.14, s32[]{:T(128)} %get-tuple-element.15, s32[]{:T(128)} %get-tuple-element.16), kind=kLoop, calls=%fused_computation.50 | loop fusion | flops 24 | bytes 36 | tf_op jit(solution)/shard_map/reduce_sum | solution.py:178
  31.2 2.5 %pad_add_fusion = (s32[2]{0:T(128)S(1)}, s32[2]{0:T(128)S(1)}) fusion(s32[1]{0:T(128)} %bitcast.7, s32[1]{0:T(128)} %bitcast.6, s32[1]{0:T(128)} %bitcast.11, s32[1]{0:T(128)} %bitcast.10), kind=kLoop, calls=%fused_computation.43 | loop fusion | flops 4 | bytes 32 | tf_op jit(solution)/shard_map/stack | solution.py:191
  33.7 0.0 collective-permute-start
  33.7 0.6 collective-permute-start.3
  34.4 6.0 %collective-permute-start.2 = (s32[2]{0:T(128)S(1)}, s32[2]{0:T(128)S(1)}, u32[]{:S(2)}, u32[]{:S(2)}) collective-permute-start(s32[2]{0:T(128)S(1)} %get-tuple-element.27), channel_id=1, source_target_pairs={{0,252},{4,0},{8,4},{12,8},{16,12},{20,16},{24,20},{28,24},{32,28}... | collective-permute-start | bytes 32 | tf_op jit(solution)/shard_map/ppermute | solution.py:19
  43.5 0.3 broadcast_in_dim.67
  43.7 4.0 %dynamic_update_slice.9 = bf16[576,2048]{1,0:T(8,128)(2,1)S(1)} dynamic-update-slice(bf16[576,2048]{1,0:T(8,128)(2,1)S(1)} %broadcast_in_dim.67, bf16[192,2048]{1,0:T(8,128)(2,1)S(1)} %get-tuple-element.18, s32[]{:T(128)S(6)} %select_n.91, s32[]{:T(128)} %constant.21.clone.1) | dynamic-update-slice | bytes 1572868 | tf_op jit(solution)/shard_map/dynamic_update_slice | solution.py:146
  47.8 0.0 collective-permute-done
  47.8 0.6 fusion.28
  49.6 0.0 collective-permute-done.2
  49.6 0.6 fusion.27
  55.3 1.8 select_select_fusion
  57.2 0.1 pad.4
  57.3 0.0 collective-permute-done.1
  57.3 1.4 dynamic-slice_add_fusion.1
  58.7 4.0 %dynamic_update_slice.10 = bf16[576,2048]{1,0:T(8,128)(2,1)S(1)} dynamic-update-slice(bf16[576,2048]{1,0:T(8,128)(2,1)S(1)} %dynamic_update_slice.9, bf16[192,2048]{1,0:T(8,128)(2,1)S(1)} %dynamic-slice_add_fusion.1, s32[]{:T(128)S(6)} %select_n.95, s32[]{:T(128)} %constant.21.clone.1) | dynamic-update-slice | bytes 1572868 | tf_op jit(solution)/shard_map/dynamic_update_slice | solution.py:146
  62.8 0.0 collective-permute-done.3
  62.8 1.4 dynamic-slice_add_fusion
  64.2 4.0 %dynamic_update_slice.11 = bf16[576,2048]{1,0:T(8,128)(2,1)S(1)} dynamic-update-slice(bf16[576,2048]{1,0:T(8,128)(2,1)S(1)} %dynamic_update_slice.10, bf16[192,2048]{1,0:T(8,128)(2,1)S(1)} %dynamic-slice_add_fusion, s32[]{:T(128)S(6)} %select_n.102, s32[]{:T(128)} %constant.21.clone.1) | dynamic-update-slice | bytes 1572868 | tf_op jit(solution)/shard_map/dynamic_update_slice | solution.py:146
  68.3 0.3 convert_reduce_fusion
  68.6 0.6 fusion.4
  69.1 85.3 %all-gather.2.cloned.1.call-done.value_ref.gate_ref = bf16[2048,6178]{1,0:T(8,128)(2,1)} async-done(((bf16[8,6178]{1,0:T(8,128)(2,1)}), bf16[2048,6178]{1,0:T(8,128)(2,1)}) %all-gather.2.cloned.1.call-update) | async-done | bytes 25305104 | tf_op jit(solution)/shard_map/all_gather | solution.py:158
  154.4 1.1 slice.47
  155.5 0.2 copy.18
  155.8 0.6 fusion.26
  156.4 0.7 slice.49.taps_ref
  157.1 1.7 fusion.6.normed_ref
  158.8 0.8 broadcast_in_dim.77.labels_ref
  159.6 39.0 %shard_map.91 = bf16[384,2048]{1,0:T(8,128)(2,1)} custom-call(bf16[384,2048]{1,0:T(8,128)(2,1)} %fusion.6.normed_ref, bf16[2048,6178]{1,0:T(8,128)(2,1)} %all-gather.2.cloned.1.call-done.value_ref.gate_ref, bf16[2048,6178]{1,0:T(8,128)(2,1)} %all-gather.2.cloned.1.call-done.value_ref.gate_ref, s32[416,128]{1,0:T(8,128)} %broadcast_in_dim.77.labels_ref, ...), custom_call_target="tpu_custom_call" | custom-call | flops 6517948416 | bytes 23068672 | tf_op jit(solution)/shard_map/pallas_call | solution.py:97
  198.7 8.4 %fusion.10 = bf16[1,384,2048]{2,1,0:T(8,128)(2,1)} fusion(bf16[384,2048]{1,0:T(8,128)(2,1)} %shard_map.91, bf16[2048,6178]{1,0:T(8,128)(2,1)} %all-gather.2.cloned.1.call-done.value_ref.gate_ref, bf16[576,2048]{1,0:T(8,128)(2,1)S(1)} %dynamic_update_slice.11), kind=kOutput, calls=%fused_computation.11 | convolution fusion | flops 3223584768 | bytes 13107200 | tf_op jit(solution)/shard_map/dot_general | solution.py:131
  (3 shorter events, 0.0 us)
Async XLA Ops:
  6.5 147.9 %all-gather.2.cloned.1.call-start = ((), (), s32[]{:S(2)}) async-start(), calls=%async_computation | async-start | bytes 25790464 | tf_op jit(solution)/shard_map/all_gather | solution.py:158
  22.4 6.2 %copy-start = (s32[1,3]{1,0:T(1,128)S(1)}, s32[1,3]{1,0:T(1,128)}, u32[]{:S(2)}) copy-start(s32[1,3]{1,0:T(1,128)} %param.12) | copy-start | bytes 40
  26.0 31.3 %collective-permute-start.1 = (bf16[192,2048]{1,0:T(8,128)(2,1)}, bf16[192,2048]{1,0:T(8,128)(2,1)}, u32[]{:S(2)}, u32[]{:S(2)}) collective-permute-start(bf16[192,2048]{1,0:T(8,128)(2,1)} %get-tuple-element.19), channel_id=1, source_target_pairs={{0,4},{4,8},{8,12},{12,16},{16,20},{20,24},{24,28},{28,32},{32,36}... | collective-permute-start | bytes 2359304 | tf_op jit(solution)/shard_map/ppermute | solution.py:19
  33.7 14.1 %collective-permute-start = (s32[2]{0:T(128)S(1)}, s32[2]{0:T(128)S(1)}, u32[]{:S(2)}, u32[]{:S(2)}) collective-permute-start(s32[2]{0:T(128)S(1)} %get-tuple-element.26), channel_id=1, source_target_pairs={{0,4},{4,8},{8,12},{12,16},{16,20},{20,24},{24,28},{28,32},{32,36}... | collective-permute-start | bytes 32 | tf_op jit(solution)/shard_map/ppermute | solution.py:19
  33.7 29.0 %collective-permute-start.3 = (bf16[192,2048]{1,0:T(8,128)(2,1)}, bf16[192,2048]{1,0:T(8,128)(2,1)}, u32[]{:S(2)}, u32[]{:S(2)}) collective-permute-start(bf16[192,2048]{1,0:T(8,128)(2,1)} %get-tuple-element.17), channel_id=1, source_target_pairs={{0,252},{4,0},{8,4},{12,8},{16,12},{20,16},{24,20},{28,24},{32,28}... | collective-permute-start | bytes 2359304 | tf_op jit(solution)/shard_map/ppermute | solution.py:19
  34.4 15.3 %collective-permute-start.2 = (s32[2]{0:T(128)S(1)}, s32[2]{0:T(128)S(1)}, u32[]{:S(2)}, u32[]{:S(2)}) collective-permute-start(s32[2]{0:T(128)S(1)} %get-tuple-element.27), channel_id=1, source_target_pairs={{0,252},{4,0},{8,4},{12,8},{16,12},{20,16},{24,20},{28,24},{32,28}... | collective-permute-start | bytes 32 | tf_op jit(solution)/shard_map/ppermute | solution.py:19
Sparse Core Ops, SparseCore 0:
  11.1 143.2 all-gather.1

commit v4 on v0

--- a/solution.py
+++ b/solution.py
@@ -1,6 +1,8 @@
 import jax
 import jax.numpy as jnp
 from jax import lax
+from jax.experimental import pallas as pl
+from jax.experimental.pallas import tpu as pltpu
 from jax.sharding import PartitionSpec as P
 
 D = 2048
@@ -34,30 +36,43 @@
     return center * lax.rsqrt(spread + epsilon) * scale_gain.astype(jnp.float32)
 
 
-def depth_pass(gated_rows, segment, depth_kernel):
+SMALL_WIDTH = 128
+
+
+def depth_pass(gated_rows, segment, taps):
     row_count = gated_rows.shape[0]
     margin = KERNEL // 2
     padded = jnp.pad(gated_rows, ((margin, margin), (0, 0)))
     labels = jnp.pad(segment, (margin, margin), constant_values=-1)
-    kernel_rows = depth_kernel.astype(jnp.float32)
     depthwise = jnp.zeros_like(gated_rows)
     for column in range(KERNEL):
         inside = (labels[column : column + row_count] == segment)[:, None]
-        depthwise = (
-            depthwise
-            + jnp.where(inside, padded[column : column + row_count], 0.0) * kernel_rows[:, column]
-        )
+        depthwise = depthwise + jnp.where(inside, padded[column : column + row_count], 0.0) * taps[column : column + 1]
     return depthwise
 
 
+def transpose_body(small_ref, out_ref):
+    out_ref[...] = jnp.transpose(small_ref[...].astype(jnp.float32))
+
+
+def small_rows(small_columns):
+    count, width = small_columns.shape
+    return pl.pallas_call(
+        transpose_body,
+        out_shape=jax.ShapeDtypeStruct((width, count), jnp.float32),
+        in_specs=[pl.BlockSpec(memory_space=pltpu.VMEM)],
+        out_specs=pl.BlockSpec(memory_space=pltpu.VMEM),
+    )(small_columns)
+
+
 def conv_module(inputs, segment, params):
-    norm_gain, weight_in, depth_kernel, post_gain, weight_out = params
+    norm_gain, weight_in, taps, post_gain, weight_out = params
     widths = inputs.shape[1]
     source = inputs.astype(jnp.float32)
     normed = layer_norm(source, norm_gain).astype(jnp.bfloat16)
     projected = jnp.dot(normed, weight_in, preferred_element_type=jnp.float32)
     gated_rows = projected[:, :widths] * jax.nn.sigmoid(projected[:, widths:])
-    depthwise = depth_pass(gated_rows, segment, depth_kernel)
+    depthwise = depth_pass(gated_rows, segment, taps)
     normed_post = layer_norm(depthwise, post_gain)
     active = (normed_post * jax.nn.sigmoid(normed_post)).astype(jnp.bfloat16)
     return (source + jnp.dot(active, weight_out, preferred_element_type=jnp.float32)).astype(
@@ -85,8 +100,18 @@
     frames, lengths, destination, offsets, norm_gain, weight_in, depth_kernel, post_gain, weight_out
 ):
     dp_count = lax.axis_size("dp")
-    params = sent_together(
-        (norm_gain, weight_in, depth_kernel, post_gain, weight_out), ("dp", "group"), 0, 1
+    small = jnp.concatenate([norm_gain[:, None], post_gain[:, None], depth_kernel], axis=1)
+    small = jnp.pad(small, ((0, 0), (0, SMALL_WIDTH - small.shape[1])))
+    both = jnp.concatenate([weight_in, weight_out, small], axis=1)
+    gathered = lax.all_gather(both, ("dp", "group"), axis=0, tiled=True)
+    columns = weight_in.shape[1] + weight_out.shape[1]
+    small_t = small_rows(gathered[:, columns:])
+    params = (
+        small_t[0:1],
+        gathered[:, : weight_in.shape[1]],
+        small_t[2 : 2 + KERNEL],
+        small_t[1:2],
+        gathered[:, weight_in.shape[1] : columns],
     )
     my_index = lax.axis_index("dp")
     local_frames = frames[0]

time: 225 us -> 210 us (0.933)
  local copies, waits for them, and re-layouts: 34.4 us -> 20.7 us
  matrix products: 21.5 us -> 18.6 us
    slice x2 -> x3, local copies, waits for them, and re-layouts: 17.5 us -> 5.51 us  [the longest x1 1.94 us: shards(): small_t = small_rows(gathered[:, columns:])]
    convert_element_type x2 -> x0, other arithmetic: 2.99 us -> none  [the longest x1 1.75 us: layer_norm(): return center * lax.rsqrt(spread + epsilon) * scale_gain.astype(jnp.float32)]
    concatenate x0 -> x2, other arithmetic: none -> 2.25 us  [the longest x1 1.5 us: shards(): both = jnp.concatenate([weight_in, weight_out, small], axis=1)]
  transfers between devices with their start and end apart: 5 -> 5, of which waited for: 1 -> 1; matrix products, arithmetic and copies ran while one was open for 16% -> 17% of each run, Pallas kernels for 0% -> 0%
where the time goes in v4:
time: 210 us; the launch traced here: 209 us
  waiting for transfers between devices  83.6 us (40%)
  other arithmetic  45.7 us (22%)
  between operations  28.6 us (14%)
  local copies, waits for them, and re-layouts  20.7 us (10%)
  matrix products  18.6 us (9%)
  starting transfers between devices  9.36 us (4%)
  Pallas kernels  2.22 us (1%)
    all_gather x1, waiting for transfers between devices, shards(): gathered = lax.all_gather(both, ('dp', 'group'), axis=0, tiled=True)  83.6 us
    reduce_sum x2, other arithmetic, layer_norm(): center = values - jnp.mean(values, axis=-1, keepdims=True)  20 us
    dynamic_update_slice x3, local copies, waits for them, and re-layouts, relocate(): lax.dynamic_update_slice_in_dim(received, current + frame_rows, meta_data...  12.1 us
    dot_general x1, matrix products, conv_module(): projected = jnp.dot(normed, weight_in, preferred_element_type=jnp.float32)  10.3 us
    ppermute x4, starting transfers between devices, shifted(): lax.ppermute(array, axis, [(i, (i + by) % peers) for i in range(peers)])  9.36 us
    dot_general x1, matrix products, conv_module(): jnp.dot(active, weight_out, preferred_element_type=jnp.float32)  8.28 us
    reduce_sum x2, other arithmetic, pick_entry(): return jnp.sum(jnp.where(slot_ids == which, values, 0))  6.59 us
  transfers between devices with their start and end apart: 5, of which 1 were waited for; matrix products, arithmetic and copies ran while one was open for 17% of the time, Pallas kernels for 0%

profile of v4, /device:TPU:1, one launch (start us, length us, event | category | flops | bytes accessed | tf_op | source)
XLA Modules:
  0.0 208.8 jit_solution(12799112791748911200)
XLA Ops:
  6.5 0.0 all-gather.2.cloned.1.call-start
  6.5 0.7 copy.11
  7.3 0.7 copy.10
  8.0 0.8 fusion.76
  8.8 1.5 pad_maximum_fusion
  10.3 0.0 all-gather.2.cloned.1.call-update
  10.3 0.8 reduce-window.9
  11.1 1.4 fusion.82
  12.5 3.3 %fusion.86 = (s32[]{:T(128)}, s32[]{:T(128)}, s32[]{:T(128)}) fusion(s32[1,3]{1,0:T(1,128)} %param.12, s32[]{:T(128)} %get-tuple-element.14, s32[]{:T(128)} %get-tuple-element.15, s32[]{:T(128)} %get-tuple-element.16), kind=kLoop, calls=%fused_computation.166 | loop fusion | flops 24 | bytes 36 | tf_op jit(solution)/shard_map/reduce_sum | solution.py:126
  15.8 3.3 %select_reduce_fusion = (s32[]{:T(128)}, s32[]{:T(128)}, s32[]{:T(128)}, s32[]{:T(128)}, s32[]{:T(128)}, /*index=5*/s32[]{:T(128)}) fusion(s32[]{:T(128)} %get-tuple-element.14, s32[1,3]{1,0:T(1,128)} %param.10, s32[3,1]{0,1:T(1,128)S(1)} %reduce-window.9, s32[]{:T(128)} %get-tuple-element.15, s32[]{:T(128)} %get-tuple-element.16), kind=kLoop, calls=%fused_computation.174 | loop fusion | flops 42 | bytes 60 | tf_op jit(solution)/shard_map/reduce_sum | solution.py:126
  19.1 2.3 %pad_add_fusion = (s32[2]{0:T(128)S(1)}, s32[2]{0:T(128)S(1)}) fusion(s32[1]{0:T(128)} %bitcast.7, s32[1]{0:T(128)} %bitcast.6, s32[1]{0:T(128)} %bitcast.11, s32[1]{0:T(128)} %bitcast.10), kind=kLoop, calls=%fused_computation.159 | loop fusion | flops 4 | bytes 32 | tf_op jit(solution)/shard_map/stack | solution.py:139
  21.4 2.7 %collective-permute-start = (s32[2]{0:T(128)S(1)}, s32[2]{0:T(128)S(1)}, u32[]{:S(2)}, u32[]{:S(2)}) collective-permute-start(s32[2]{0:T(128)S(1)} %get-tuple-element.91), channel_id=1, source_target_pairs={{0,4},{4,8},{8,12},{12,16},{16,20},{20,24},{24,28},{28,32},{32,36}... | collective-permute-start | bytes 32 | tf_op jit(solution)/shard_map/ppermute | solution.py:19
  24.1 0.6 collective-permute-start.2
  30.2 0.6 iota_compare_fusion.9
  30.8 1.1 iota_compare_fusion.7
  32.0 3.5 %bitcast_select_fusion = (bf16[192,2048]{1,0:T(8,128)(2,1)}, bf16[192,2048]{1,0:T(8,128)(2,1)S(1)}, bf16[192,2048]{1,0:T(8,128)(2,1)}) fusion(bf16[1,576,2048]{2,1,0:T(8,128)(2,1)} %param.9, s32[]{:T(128)S(6)} %select_n.199, pred[192]{0:T(512)(128)(4,1)S(1)} %get-tuple-element.93, s32[]{:T(128)S(6)} %select_n.183, pred[192]{0:T(512)(128)(4,1)S(1)} %iota_compare_fusion.9, ...), kind=kLoop, calls=%fused_computation.89 | loop fusion | flops 1179648 | bytes 4719180 | tf_op jit(solution)/shard_map/jit(_where)/select_n | solution.py:138
  35.5 1.1 collective-permute-start.1
  36.6 4.9 %collective-permute-start.3 = (bf16[192,2048]{1,0:T(8,128)(2,1)}, bf16[192,2048]{1,0:T(8,128)(2,1)}, u32[]{:S(2)}, u32[]{:S(2)}) collective-permute-start(bf16[192,2048]{1,0:T(8,128)(2,1)} %get-tuple-element.19), channel_id=1, source_target_pairs={{0,252},{4,0},{8,4},{12,8},{16,12},{20,16},{24,20},{28,24},{32,28}... | collective-permute-start | bytes 2359304 | tf_op jit(solution)/shard_map/ppermute | solution.py:19
  44.5 0.3 broadcast_in_dim.291
  44.8 4.0 %dynamic_update_slice.9 = bf16[576,2048]{1,0:T(8,128)(2,1)S(1)} dynamic-update-slice(bf16[576,2048]{1,0:T(8,128)(2,1)S(1)} %broadcast_in_dim.291, bf16[192,2048]{1,0:T(8,128)(2,1)S(1)} %get-tuple-element.20, s32[]{:T(128)S(6)} %select_n.186, s32[]{:T(128)} %constant.48.clone.1) | dynamic-update-slice | bytes 1572868 | tf_op jit(solution)/shard_map/dynamic_update_slice | solution.py:93
  48.9 0.0 collective-permute-done
  48.9 0.6 fusion.95
  50.8 0.0 collective-permute-done.2
  50.8 0.7 fusion.94
  52.8 1.9 select_select_fusion
  54.7 0.1 slice_compare_fusion.30
  54.8 0.1 slice_compare_fusion.29
  54.9 0.1 slice_compare_fusion.27
  58.9 0.1 slice_compare_fusion.28
  59.0 0.0 collective-permute-done.1
  59.0 1.4 dynamic-slice_add_fusion.1
  60.4 4.0 %dynamic_update_slice.10 = bf16[576,2048]{1,0:T(8,128)(2,1)S(1)} dynamic-update-slice(bf16[576,2048]{1,0:T(8,128)(2,1)S(1)} %dynamic_update_slice.9, bf16[192,2048]{1,0:T(8,128)(2,1)S(1)} %dynamic-slice_add_fusion.1, s32[]{:T(128)S(6)} %select_n.190, s32[]{:T(128)} %constant.48.clone.1) | dynamic-update-slice | bytes 1572868 | tf_op jit(solution)/shard_map/dynamic_update_slice | solution.py:93
  64.5 0.0 collective-permute-done.3
  64.5 1.4 dynamic-slice_add_fusion
  65.9 4.0 %dynamic_update_slice.11 = bf16[576,2048]{1,0:T(8,128)(2,1)S(1)} dynamic-update-slice(bf16[576,2048]{1,0:T(8,128)(2,1)S(1)} %dynamic_update_slice.10, bf16[192,2048]{1,0:T(8,128)(2,1)S(1)} %dynamic-slice_add_fusion, s32[]{:T(128)S(6)} %select_n.197, s32[]{:T(128)} %constant.48.clone.1) | dynamic-update-slice | bytes 1572868 | tf_op jit(solution)/shard_map/dynamic_update_slice | solution.py:93
  70.0 0.3 convert_reduce_fusion
  70.3 0.6 fusion.6
  70.8 83.6 %all-gather.2.cloned.1.call-done = bf16[2048,6272]{1,0:T(8,128)(2,1)} async-done(((bf16[8,6272]{1,0:T(8,128)(2,1)}), bf16[2048,6272]{1,0:T(8,128)(2,1)}) %all-gather.2.cloned.1.call-update) | async-done | bytes 25690128 | tf_op jit(solution)/shard_map/all_gather | solution.py:106
  154.5 1.9 slice.466.small_ref
  156.4 2.2 %shard_map.91 = f32[128,2048]{1,0:T(8,128)} custom-call(bf16[2048,128]{1,0:T(8,128)(2,1)} %slice.466.small_ref), custom_call_target="tpu_custom_call" | custom-call | tf_op jit(solution)/shard_map/pallas_call | solution.py:60
  158.6 1.7 fusion.92
  160.3 1.8 fusion.93
  162.2 10.3 %fusion = f32[384,4096]{1,0:T(8,128)S(1)} fusion(bf16[2048,6272]{1,0:T(8,128)(2,1)} %all-gather.2.cloned.1.call-done, f32[2048]{0:T(1024)S(1)} %bitcast.123, f32[384]{0:T(512)S(1)} %add_rsqrt_fusion.1, f32[384]{0:T(512)S(1)} %broadcast_multiply_fusion.1, bf16[576,2048]{1,0:T(8,128)(2,1)S(1)} %dynamic_update_slice.11), kind=kOutput, calls=%fused_computation | convolution fusion | flops 6446383104 | bytes 24653824 | tf_op jit(solution)/shard_map/dot_general | solution.py:73
  172.5 1.0 fusion.13
  173.5 19.7 %fusion.91 = (f32[384]{0:T(512)S(1)}, f32[384,2048]{1,0:T(8,128)S(1)}) fusion(f32[2048]{0:T(1024)S(1)} %bitcast.90, pred[384]{0:T(512)(128)(4,1)S(1)} %get-tuple-element.86, f32[2048]{0:T(1024)S(1)} %bitcast.91, pred[384]{0:T(512)(128)(4,1)S(1)} %get-tuple-element.57, f32[2048]{0:T(1024)S(1)} %bitcast.92, pred[384]{0:T(512)(128)(4,1)S(1)} %get-tuple-element.58, ...), kind=kLoop, calls=%fused_computation.181 | loop fusion | flops 74710656 | bytes 6567040 | tf_op jit(solution)/shard_map/reduce_sum | solution.py:34
  193.2 0.5 multiply_reduce_fusion
  193.7 8.3 %fusion.60 = bf16[1,384,2048]{2,1,0:T(8,128)(2,1)} fusion(bf16[2048,6272]{1,0:T(8,128)(2,1)} %all-gather.2.cloned.1.call-done, f32[384,2048]{1,0:T(8,128)S(1)} %get-tuple-element.18, f32[2048]{0:T(1024)S(1)} %bitcast.122, f32[384]{0:T(512)S(1)} %add_rsqrt_fusion, f32[384]{0:T(512)S(1)} %broadcast_multiply_fusion, bf16[576,2048]{1,0:T(8,128)(2,1)S(1)} %dynamic_update_slice.11), kind=kOutput, calls=%fused_computation.80 | convolution fusion | flops 3229876224 | bytes 14691328 | tf_op jit(solution)/shard_map/dot_general | solution.py:78
  (4 shorter events, 0.0 us)
Async XLA Ops:
  6.5 147.9 %all-gather.2.cloned.1.call-start = ((), (), s32[]{:S(2)}) async-start(), calls=%async_computation | async-start | bytes 25790464 | tf_op jit(solution)/shard_map/all_gather | solution.py:106
  21.4 27.5 %collective-permute-start = (s32[2]{0:T(128)S(1)}, s32[2]{0:T(128)S(1)}, u32[]{:S(2)}, u32[]{:S(2)}) collective-permute-start(s32[2]{0:T(128)S(1)} %get-tuple-element.91), channel_id=1, source_target_pairs={{0,4},{4,8},{8,12},{12,16},{16,20},{20,24},{24,28},{28,32},{32,36}... | collective-permute-start | bytes 32 | tf_op jit(solution)/shard_map/ppermute | solution.py:19
  24.1 26.7 %collective-permute-start.2 = (s32[2]{0:T(128)S(1)}, s32[2]{0:T(128)S(1)}, u32[]{:S(2)}, u32[]{:S(2)}) collective-permute-start(s32[2]{0:T(128)S(1)} %get-tuple-element.92), channel_id=1, source_target_pairs={{0,252},{4,0},{8,4},{12,8},{16,12},{20,16},{24,20},{28,24},{32,28}... | collective-permute-start | bytes 32 | tf_op jit(solution)/shard_map/ppermute | solution.py:19
  35.5 23.5 %collective-permute-start.1 = (bf16[192,2048]{1,0:T(8,128)(2,1)}, bf16[192,2048]{1,0:T(8,128)(2,1)}, u32[]{:S(2)}, u32[]{:S(2)}) collective-permute-start(bf16[192,2048]{1,0:T(8,128)(2,1)} %get-tuple-element.21), channel_id=1, source_target_pairs={{0,4},{4,8},{8,12},{12,16},{16,20},{20,24},{24,28},{28,32},{32,36}... | collective-permute-start | bytes 2359304 | tf_op jit(solution)/shard_map/ppermute | solution.py:19
  36.6 27.9 %collective-permute-start.3 = (bf16[192,2048]{1,0:T(8,128)(2,1)}, bf16[192,2048]{1,0:T(8,128)(2,1)}, u32[]{:S(2)}, u32[]{:S(2)}) collective-permute-start(bf16[192,2048]{1,0:T(8,128)(2,1)} %get-tuple-element.19), channel_id=1, source_target_pairs={{0,252},{4,0},{8,4},{12,8},{16,12},{20,16},{24,20},{28,24},{32,28}... | collective-permute-start | bytes 2359304 | tf_op jit(solution)/shard_map/ppermute | solution.py:19
Sparse Core Ops, SparseCore 0:
  11.1 143.2 all-gather.1

commit v5 on v4

--- a/solution.py
+++ b/solution.py
@@ -102,10 +102,13 @@
     dp_count = lax.axis_size("dp")
     small = jnp.concatenate([norm_gain[:, None], post_gain[:, None], depth_kernel], axis=1)
     small = jnp.pad(small, ((0, 0), (0, SMALL_WIDTH - small.shape[1])))
-    both = jnp.concatenate([weight_in, weight_out, small], axis=1)
+    both = jnp.concatenate([weight_in, weight_out], axis=1)
     gathered = lax.all_gather(both, ("dp", "group"), axis=0, tiled=True)
     columns = weight_in.shape[1] + weight_out.shape[1]
-    small_t = small_rows(gathered[:, columns:])
+    peers = lax.axis_size(("dp", "group"))
+    copies = jnp.broadcast_to(small[None], (peers,) + small.shape)
+    spread = lax.all_to_all(copies, ("dp", "group"), 0, 0, tiled=True)
+    small_t = small_rows(spread.reshape(-1, SMALL_WIDTH))
     params = (
         small_t[0:1],
         gathered[:, : weight_in.shape[1]],

time: 210 us -> 203 us (0.967)
  waiting for transfers between devices: 83.6 us -> 63.7 us
  starting transfers between devices: 9.36 us -> 24 us
    all_gather x1, waiting for transfers between devices: 83.6 us -> 63.6 us  [shards(): gathered = lax.all_gather(both, ('dp', 'group'), axis=0, tiled=True)]
    all_to_all x0 -> x1, starting transfers between devices: none -> 16.7 us  [shards(): spread = lax.all_to_all(copies, ('dp', 'group'), 0, 0, tiled=True)]
  transfers between devices with their start and end apart: 5 -> 6, of which waited for: 1 -> 1; matrix products, arithmetic and copies ran while one was open for 17% -> 21% of each run, Pallas kernels for 0% -> 1%
where the time goes in v5:
time: 203 us; the launch traced here: 202 us
  waiting for transfers between devices  63.7 us (31%)
  other arithmetic  45.8 us (23%)
  between operations  28.3 us (14%)
  starting transfers between devices  24 us (12%)
  local copies, waits for them, and re-layouts  19.6 us (10%)
  matrix products  18.6 us (9%)
  Pallas kernels  2.22 us (1%)
    all_gather x1, waiting for transfers between devices, shards(): gathered = lax.all_gather(both, ('dp', 'group'), axis=0, tiled=True)  63.6 us
    reduce_sum x2, other arithmetic, layer_norm(): center = values - jnp.mean(values, axis=-1, keepdims=True)  20 us
    all_to_all x1, starting transfers between devices, shards(): spread = lax.all_to_all(copies, ('dp', 'group'), 0, 0, tiled=True)  16.7 us
    dynamic_update_slice x3, local copies, waits for them, and re-layouts, relocate(): lax.dynamic_update_slice_in_dim(received, current + frame_rows, meta_data...  12.1 us
    dot_general x1, matrix products, conv_module(): projected = jnp.dot(normed, weight_in, preferred_element_type=jnp.float32)  10.3 us
    dot_general x1, matrix products, conv_module(): jnp.dot(active, weight_out, preferred_element_type=jnp.float32)  8.28 us
    ppermute x4, starting transfers between devices, shifted(): lax.ppermute(array, axis, [(i, (i + by) % peers) for i in range(peers)])  7.29 us
    reduce_sum x2, other arithmetic, pick_entry(): return jnp.sum(jnp.where(slot_ids == which, values, 0))  6.4 us
  transfers between devices with their start and end apart: 6, of which 1 were waited for; matrix products, arithmetic and copies ran while one was open for 21% of the time, Pallas kernels for 1%

profile of v5, /device:TPU:1, one launch (start us, length us, event | category | flops | bytes accessed | tf_op | source)
XLA Modules:
  0.0 202.2 jit_solution(17709543313402085162)
XLA Ops:
  6.5 1.5 pad_maximum_fusion
  8.0 0.0 all-gather.2.cloned.1.call-update
  8.1 0.7 copy.11
  8.8 0.7 copy.10
  9.5 0.8 fusion.76
  10.3 0.9 broadcast_in_dim.308
  11.2 16.7 %all-to-all-start = ((bf16[256,8,128]{2,1,0:T(8,128)(2,1)}), bf16[256,8,128]{2,1,0:T(8,128)(2,1)}, u32[]{:S(2)}, u32[]{:S(2)}) async-start(bf16[256,8,128]{2,1,0:T(8,128)(2,1)} %broadcast_in_dim.308), calls=%async_computation | async-start | bytes 1048576 | tf_op jit(solution)/shard_map/all_to_all | solution.py:110
  27.8 0.8 reduce-window.9
  28.7 1.3 fusion.82
  30.0 3.2 %fusion.86 = (s32[]{:T(128)}, s32[]{:T(128)}, s32[]{:T(128)}) fusion(s32[1,3]{1,0:T(1,128)} %param.12, s32[]{:T(128)} %get-tuple-element.14, s32[]{:T(128)} %get-tuple-element.15, s32[]{:T(128)} %get-tuple-element.16), kind=kLoop, calls=%fused_computation.166 | loop fusion | flops 24 | bytes 36 | tf_op jit(solution)/shard_map/reduce_sum | solution.py:129
  33.2 3.2 %select_reduce_fusion = (s32[]{:T(128)}, s32[]{:T(128)}, s32[]{:T(128)}, s32[]{:T(128)}, s32[]{:T(128)}, /*index=5*/s32[]{:T(128)}) fusion(s32[]{:T(128)} %get-tuple-element.14, s32[1,3]{1,0:T(1,128)} %param.10, s32[3,1]{0,1:T(1,128)S(1)} %reduce-window.9, s32[]{:T(128)} %get-tuple-element.15, s32[]{:T(128)} %get-tuple-element.16), kind=kLoop, calls=%fused_computation.174 | loop fusion | flops 42 | bytes 60 | tf_op jit(solution)/shard_map/reduce_sum | solution.py:129
  36.4 2.5 %pad_add_fusion = (s32[2]{0:T(128)S(1)}, s32[2]{0:T(128)S(1)}) fusion(s32[1]{0:T(128)} %bitcast.7, s32[1]{0:T(128)} %bitcast.6, s32[1]{0:T(128)} %bitcast.11, s32[1]{0:T(128)} %bitcast.10), kind=kLoop, calls=%fused_computation.159 | loop fusion | flops 4 | bytes 32 | tf_op jit(solution)/shard_map/stack | solution.py:142
  38.9 1.7 collective-permute-start
  40.6 0.7 collective-permute-start.2
  46.8 0.6 iota_compare_fusion.9
  47.5 1.2 iota_compare_fusion.7
  48.7 3.5 %bitcast_select_fusion = (bf16[192,2048]{1,0:T(8,128)(2,1)}, bf16[192,2048]{1,0:T(8,128)(2,1)S(1)}, bf16[192,2048]{1,0:T(8,128)(2,1)}) fusion(bf16[1,576,2048]{2,1,0:T(8,128)(2,1)} %param.9, s32[]{:T(128)S(6)} %select_n.199, pred[192]{0:T(512)(128)(4,1)S(1)} %get-tuple-element.93, s32[]{:T(128)S(6)} %select_n.183, pred[192]{0:T(512)(128)(4,1)S(1)} %iota_compare_fusion.9, ...), kind=kLoop, calls=%fused_computation.89 | loop fusion | flops 1179648 | bytes 4719180 | tf_op jit(solution)/shard_map/jit(_where)/select_n | solution.py:141
  52.2 1.1 collective-permute-start.1
  53.3 3.9 %collective-permute-start.3 = (bf16[192,2048]{1,0:T(8,128)(2,1)}, bf16[192,2048]{1,0:T(8,128)(2,1)}, u32[]{:S(2)}, u32[]{:S(2)}) collective-permute-start(bf16[192,2048]{1,0:T(8,128)(2,1)} %get-tuple-element.19), channel_id=1, source_target_pairs={{0,252},{4,0},{8,4},{12,8},{16,12},{20,16},{24,20},{28,24},{32,28}... | collective-permute-start | bytes 2359304 | tf_op jit(solution)/shard_map/ppermute | solution.py:19
  60.1 0.3 broadcast_in_dim.297
  60.4 4.0 %dynamic_update_slice.9 = bf16[576,2048]{1,0:T(8,128)(2,1)S(1)} dynamic-update-slice(bf16[576,2048]{1,0:T(8,128)(2,1)S(1)} %broadcast_in_dim.297, bf16[192,2048]{1,0:T(8,128)(2,1)S(1)} %get-tuple-element.20, s32[]{:T(128)S(6)} %select_n.186, s32[]{:T(128)} %constant.48.clone.1) | dynamic-update-slice | bytes 1572868 | tf_op jit(solution)/shard_map/dynamic_update_slice | solution.py:93
  64.4 0.0 collective-permute-done
  64.4 0.6 fusion.95
  66.3 0.0 collective-permute-done.2
  66.3 0.6 fusion.94
  68.2 1.8 select_select_fusion
  70.0 0.1 slice_compare_fusion.30
  70.1 0.1 slice_compare_fusion.29
  70.2 0.1 slice_compare_fusion.27
  74.1 0.1 slice_compare_fusion.28
  74.2 0.0 collective-permute-done.1
  74.2 1.4 dynamic-slice_add_fusion.1
  75.6 4.0 %dynamic_update_slice.10 = bf16[576,2048]{1,0:T(8,128)(2,1)S(1)} dynamic-update-slice(bf16[576,2048]{1,0:T(8,128)(2,1)S(1)} %dynamic_update_slice.9, bf16[192,2048]{1,0:T(8,128)(2,1)S(1)} %dynamic-slice_add_fusion.1, s32[]{:T(128)S(6)} %select_n.190, s32[]{:T(128)} %constant.48.clone.1) | dynamic-update-slice | bytes 1572868 | tf_op jit(solution)/shard_map/dynamic_update_slice | solution.py:93
  79.7 0.0 collective-permute-done.3
  79.7 1.4 dynamic-slice_add_fusion
  81.2 4.0 %dynamic_update_slice.11 = bf16[576,2048]{1,0:T(8,128)(2,1)S(1)} dynamic-update-slice(bf16[576,2048]{1,0:T(8,128)(2,1)S(1)} %dynamic_update_slice.10, bf16[192,2048]{1,0:T(8,128)(2,1)S(1)} %dynamic-slice_add_fusion, s32[]{:T(128)S(6)} %select_n.197, s32[]{:T(128)} %constant.48.clone.1) | dynamic-update-slice | bytes 1572868 | tf_op jit(solution)/shard_map/dynamic_update_slice | solution.py:93
  85.2 0.3 convert_reduce_fusion
  85.5 0.6 fusion.6
  86.1 0.0 all-to-all-done
  86.1 2.2 %shard_map.91 = f32[128,2048]{1,0:T(8,128)} custom-call(bf16[2048,128]{1,0:T(8,128)(2,1)} %bitcast.18.small_ref), custom_call_target="tpu_custom_call" | custom-call | tf_op jit(solution)/shard_map/pallas_call | solution.py:60
  88.3 1.8 fusion.93
  90.1 1.7 fusion.92
  91.9 63.6 %all-gather.2.cloned.1.call-done = bf16[2048,6144]{1,0:T(8,128)(2,1)} async-done(((bf16[8,6144]{1,0:T(8,128)(2,1)}), bf16[2048,6144]{1,0:T(8,128)(2,1)}) %all-gather.2.cloned.1.call-update) | async-done | bytes 25165840 | tf_op jit(solution)/shard_map/all_gather | solution.py:106
  155.5 10.3 %fusion = f32[384,4096]{1,0:T(8,128)S(1)} fusion(bf16[2048,6144]{1,0:T(8,128)(2,1)} %all-gather.2.cloned.1.call-done, f32[2048]{0:T(1024)S(1)} %bitcast.124, f32[384]{0:T(512)S(1)} %add_rsqrt_fusion.1, f32[384]{0:T(512)S(1)} %broadcast_multiply_fusion.1, bf16[576,2048]{1,0:T(8,128)(2,1)S(1)} %dynamic_update_slice.11), kind=kOutput, calls=%fused_computation | convolution fusion | flops 6446383104 | bytes 24653824 | tf_op jit(solution)/shard_map/dot_general | solution.py:73
  165.9 1.0 fusion.13
  166.9 19.7 %fusion.91 = (f32[384]{0:T(512)S(1)}, f32[384,2048]{1,0:T(8,128)S(1)}) fusion(f32[2048]{0:T(1024)S(1)} %bitcast.105, pred[384]{0:T(512)(128)(4,1)S(1)} %get-tuple-element.86, f32[2048]{0:T(1024)S(1)} %bitcast.106, pred[384]{0:T(512)(128)(4,1)S(1)} %get-tuple-element.57, f32[2048]{0:T(1024)S(1)} %bitcast.107, pred[384]{0:T(512)(128)(4,1)S(1)} %get-tuple-element.58, ...), kind=kLoop, calls=%fused_computation.181 | loop fusion | flops 74710656 | bytes 6567040 | tf_op jit(solution)/shard_map/reduce_sum | solution.py:34
  186.6 0.5 multiply_reduce_fusion
  187.0 8.3 %fusion.60 = bf16[1,384,2048]{2,1,0:T(8,128)(2,1)} fusion(bf16[2048,6144]{1,0:T(8,128)(2,1)} %all-gather.2.cloned.1.call-done, f32[384,2048]{1,0:T(8,128)S(1)} %get-tuple-element.18, f32[2048]{0:T(1024)S(1)} %bitcast.123, f32[384]{0:T(512)S(1)} %add_rsqrt_fusion, f32[384]{0:T(512)S(1)} %broadcast_multiply_fusion, bf16[576,2048]{1,0:T(8,128)(2,1)S(1)} %dynamic_update_slice.11), kind=kOutput, calls=%fused_computation.80 | convolution fusion | flops 3229876224 | bytes 14691328 | tf_op jit(solution)/shard_map/dot_general | solution.py:78
  (5 shorter events, 0.0 us)
Async XLA Ops:
  6.5 149.0 %all-gather.2.cloned.1.call-start = ((), (), s32[]{:S(2)}) async-start(), calls=%async_computation.1 | async-start | bytes 25264128 | tf_op jit(solution)/shard_map/all_gather | solution.py:106
  11.2 74.9 %all-to-all-start = ((bf16[256,8,128]{2,1,0:T(8,128)(2,1)}), bf16[256,8,128]{2,1,0:T(8,128)(2,1)}, u32[]{:S(2)}, u32[]{:S(2)}) async-start(bf16[256,8,128]{2,1,0:T(8,128)(2,1)} %broadcast_in_dim.308), calls=%async_computation | async-start | bytes 1048576 | tf_op jit(solution)/shard_map/all_to_all | solution.py:110
  38.9 25.5 %collective-permute-start = (s32[2]{0:T(128)S(1)}, s32[2]{0:T(128)S(1)}, u32[]{:S(2)}, u32[]{:S(2)}) collective-permute-start(s32[2]{0:T(128)S(1)} %get-tuple-element.91), channel_id=1, source_target_pairs={{0,4},{4,8},{8,12},{12,16},{16,20},{20,24},{24,28},{28,32},{32,36}... | collective-permute-start | bytes 32 | tf_op jit(solution)/shard_map/ppermute | solution.py:19
  40.6 25.7 %collective-permute-start.2 = (s32[2]{0:T(128)S(1)}, s32[2]{0:T(128)S(1)}, u32[]{:S(2)}, u32[]{:S(2)}) collective-permute-start(s32[2]{0:T(128)S(1)} %get-tuple-element.92), channel_id=1, source_target_pairs={{0,252},{4,0},{8,4},{12,8},{16,12},{20,16},{24,20},{28,24},{32,28}... | collective-permute-start | bytes 32 | tf_op jit(solution)/shard_map/ppermute | solution.py:19
  52.2 22.0 %collective-permute-start.1 = (bf16[192,2048]{1,0:T(8,128)(2,1)}, bf16[192,2048]{1,0:T(8,128)(2,1)}, u32[]{:S(2)}, u32[]{:S(2)}) collective-permute-start(bf16[192,2048]{1,0:T(8,128)(2,1)} %get-tuple-element.21), channel_id=1, source_target_pairs={{0,4},{4,8},{8,12},{12,16},{16,20},{20,24},{24,28},{28,32},{32,36}... | collective-permute-start | bytes 2359304 | tf_op jit(solution)/shard_map/ppermute | solution.py:19
  53.3 26.4 %collective-permute-start.3 = (bf16[192,2048]{1,0:T(8,128)(2,1)}, bf16[192,2048]{1,0:T(8,128)(2,1)}, u32[]{:S(2)}, u32[]{:S(2)}) collective-permute-start(bf16[192,2048]{1,0:T(8,128)(2,1)} %get-tuple-element.19), channel_id=1, source_target_pairs={{0,252},{4,0},{8,4},{12,8},{16,12},{20,16},{24,20},{28,24},{32,28}... | collective-permute-start | bytes 2359304 | tf_op jit(solution)/shard_map/ppermute | solution.py:19
Sparse Core Ops, SparseCore 0:
  11.2 144.2 all-gather.1

commit v6 on v5

--- a/solution.py
+++ b/solution.py
@@ -39,15 +39,24 @@
 SMALL_WIDTH = 128
 
 
-def depth_pass(gated_rows, segment, taps):
+def depth_pass(gated_rows, segment, taps, bounds):
     row_count = gated_rows.shape[0]
     margin = KERNEL // 2
     padded = jnp.pad(gated_rows, ((margin, margin), (0, 0)))
     labels = jnp.pad(segment, (margin, margin), constant_values=-1)
     depthwise = jnp.zeros_like(gated_rows)
     for column in range(KERNEL):
-        inside = (labels[column : column + row_count] == segment)[:, None]
-        depthwise = depthwise + jnp.where(inside, padded[column : column + row_count], 0.0) * taps[column : column + 1]
+        depthwise = depthwise + padded[column : column + row_count] * taps[column : column + 1]
+    for bound in bounds:
+        start = bound - margin
+        window = lax.dynamic_slice_in_dim(padded, start, 2 * KERNEL, 0)
+        window_labels = lax.dynamic_slice_in_dim(labels, start, 2 * KERNEL, 0)
+        own = lax.dynamic_slice_in_dim(segment, start, KERNEL, 0)
+        exact = jnp.zeros((KERNEL, gated_rows.shape[1]), gated_rows.dtype)
+        for column in range(KERNEL):
+            inside = (window_labels[column : column + KERNEL] == own)[:, None]
+            exact = exact + jnp.where(inside, window[column : column + KERNEL], 0.0) * taps[column : column + 1]
+        depthwise = lax.dynamic_update_slice_in_dim(depthwise, exact, start, 0)
     return depthwise
 
 
@@ -65,16 +74,16 @@
     )(small_columns)
 
 
-def conv_module(inputs, segment, params):
+def conv_module(inputs, segment, bounds, params):
     norm_gain, weight_in, taps, post_gain, weight_out = params
     widths = inputs.shape[1]
     source = inputs.astype(jnp.float32)
     normed = layer_norm(source, norm_gain).astype(jnp.bfloat16)
     projected = jnp.dot(normed, weight_in, preferred_element_type=jnp.float32)
     gated_rows = projected[:, :widths] * jax.nn.sigmoid(projected[:, widths:])
-    depthwise = depth_pass(gated_rows, segment, taps)
+    depthwise = depth_pass(gated_rows, segment, taps, bounds)
     normed_post = layer_norm(depthwise, post_gain)
-    active = (normed_post * jax.nn.sigmoid(normed_post)).astype(jnp.bfloat16)
+    active = lax.optimization_barrier((normed_post * jax.nn.sigmoid(normed_post)).astype(jnp.bfloat16))
     return (source + jnp.dot(active, weight_out, preferred_element_type=jnp.float32)).astype(
         jnp.bfloat16
     )
@@ -93,7 +102,8 @@
         received = lax.dynamic_update_slice_in_dim(received, current + frame_rows, meta_data[1], 0)
         inside = (position >= meta_data[1]) & (position < meta_data[1] + meta_data[0])
         segment = jnp.where(inside, label_id + 1, segment)
-    return (received[:RCV_DEV], segment)
+    ordered = jnp.sort(jnp.stack([meta[1] for _, meta in arrivals]))
+    return (received[:RCV_DEV], segment, (ordered[1], ordered[2]))
 
 
 def shards(
@@ -141,12 +151,12 @@
         kept = jnp.where(keep_rows[:, None], frame_rows, jnp.zeros_like(frame_rows))
         return (kept, jnp.stack([live_count, pick_entry(offsets_here, which)]))
 
-    received, segment = relocate(
+    received, segment, bounds = relocate(
         cut_utterance(local_frames, chosen[0]),
         cut_utterance(local_frames, chosen[1]),
         cut_utterance(local_frames, chosen[2]),
     )
-    mixed = conv_module(received, segment, params)
+    mixed = conv_module(received, segment, bounds, params)
     return mixed[None]
 
 

time: 203 us -> 214 us (1.054)
  other arithmetic: 45.8 us -> 59.1 us
  waiting for transfers between devices: 63.7 us -> 52.4 us
  local copies, waits for them, and re-layouts: 19.6 us -> 25.6 us
  between operations: 28.3 us -> 34 us
  starting transfers between devices: 24 us -> 21.3 us
    add x0 -> x3, other arithmetic: none -> 23 us  [the longest x1 13.1 us: depth_pass(): depthwise + padded[column:column + row_count] * taps[column:column + 1]]
    reduce_sum x2, other arithmetic: 20 us -> 2.55 us  [layer_norm(): center = values - jnp.mean(values, axis=-1, keepdims=True)]
    all_gather x1, waiting for transfers between devices: 63.6 us -> 52.4 us  [shards(): gathered = lax.all_gather(both, ('dp', 'group'), axis=0, tiled=True)]
    dynamic_update_slice x0 -> x2, local copies, waits for them, and re-layouts: none -> 3.67 us  [depth_pass(): depthwise = lax.dynamic_update_slice_in_dim(depthwise, exact, start, 0)]
    eq x4 -> x5, other arithmetic: 0.33 us -> 3.55 us  [depth_pass(): inside = (window_labels[column:column + KERNEL] == own)[:, None]]
  transfers between devices with their start and end apart: 6 -> 6, of which waited for: 1 -> 1; matrix products, arithmetic and copies ran while one was open for 21% -> 24% of each run, Pallas kernels for 1% -> 1%
where the time goes in v6:
time: 214 us; the launch traced here: 213 us
  other arithmetic  59.1 us (28%)
  waiting for transfers between devices  52.4 us (24%)
  between operations  34 us (16%)
  local copies, waits for them, and re-layouts  25.6 us (12%)
  starting transfers between devices  21.3 us (10%)
  matrix products  18.3 us (9%)
  Pallas kernels  2.22 us (1%)
    all_gather x1, waiting for transfers between devices, shards(): gathered = lax.all_gather(both, ('dp', 'group'), axis=0, tiled=True)  52.4 us
    all_to_all x1, starting transfers between devices, shards(): spread = lax.all_to_all(copies, ('dp', 'group'), 0, 0, tiled=True)  15.8 us
    add x1, other arithmetic, depth_pass(): depthwise + padded[column:column + row_count] * taps[column:column + 1]  13.1 us
    dynamic_update_slice x3, local copies, waits for them, and re-layouts, relocate(): lax.dynamic_update_slice_in_dim(received, current + frame_rows, meta_data...  12.1 us
    dot_general x1, matrix products, conv_module(): projected = jnp.dot(normed, weight_in, preferred_element_type=jnp.float32)  10.3 us
    add x2, other arithmetic, depth_pass(): exact + jnp.where(inside, window[column:column + KERNEL], 0.0) * taps[col...  9.83 us
    dot_general x1, matrix products, conv_module(): jnp.dot(active, weight_out, preferred_element_type=jnp.float32)  7.98 us
    reduce_sum x2, other arithmetic, pick_entry(): return jnp.sum(jnp.where(slot_ids == which, values, 0))  6.62 us
  transfers between devices with their start and end apart: 6, of which 1 were waited for; matrix products, arithmetic and copies ran while one was open for 24% of the time, Pallas kernels for 1%

profile of v6, /device:TPU:1, one launch (start us, length us, event | category | flops | bytes accessed | tf_op | source)
XLA Modules:
  0.0 213.0 jit_solution(1207338418827761680)
XLA Ops:
  6.5 1.5 pad_maximum_fusion
  8.1 0.8 reduce-window.9
  8.9 1.4 fusion.224
  10.3 3.3 %fusion.228 = (s32[]{:T(128)}, s32[]{:T(128)}, s32[]{:T(128)}) fusion(s32[1,3]{1,0:T(1,128)} %param.12, s32[]{:T(128)} %get-tuple-element.17, s32[]{:T(128)} %get-tuple-element.18, s32[]{:T(128)} %get-tuple-element.19), kind=kLoop, calls=%fused_computation.329 | loop fusion | flops 24 | bytes 36 | tf_op jit(solution)/shard_map/reduce_sum | solution.py:139
  13.6 3.3 %select_reduce_fusion = (s32[]{:T(128)}, s32[]{:T(128)}, s32[]{:T(128)}, s32[]{:T(128)}, s32[]{:T(128)}, /*index=5*/s32[]{:T(128)}) fusion(s32[]{:T(128)} %get-tuple-element.17, s32[1,3]{1,0:T(1,128)} %param.10, s32[3,1]{0,1:T(1,128)S(1)} %reduce-window.9, s32[]{:T(128)} %get-tuple-element.18, s32[]{:T(128)} %get-tuple-element.19), kind=kLoop, calls=%fused_computation.401 | loop fusion | flops 42 | bytes 60 | tf_op jit(solution)/shard_map/reduce_sum | solution.py:139
  16.9 2.6 %pad_add_fusion = (s32[2]{0:T(128)S(1)}, s32[2]{0:T(128)S(1)}) fusion(s32[1]{0:T(128)} %bitcast.7, s32[1]{0:T(128)} %bitcast.6, s32[1]{0:T(128)} %bitcast.11, s32[1]{0:T(128)} %bitcast.10), kind=kLoop, calls=%fused_computation.321 | loop fusion | flops 4 | bytes 32 | tf_op jit(solution)/shard_map/stack | solution.py:152
  19.5 2.7 %collective-permute-start = (s32[2]{0:T(128)S(1)}, s32[2]{0:T(128)S(1)}, u32[]{:S(2)}, u32[]{:S(2)}) collective-permute-start(s32[2]{0:T(128)S(1)} %get-tuple-element.133), channel_id=1, source_target_pairs={{0,4},{4,8},{8,12},{12,16},{16,20},{20,24},{24,28},{28,32},{32,36}... | collective-permute-start | bytes 32 | tf_op jit(solution)/shard_map/ppermute | solution.py:19
  22.2 0.6 collective-permute-start.2
  22.8 0.7 copy.10
  23.6 0.7 copy.11
  24.3 0.8 fusion.218
  25.1 0.9 broadcast_in_dim.529
  25.9 15.8 %all-to-all-start = ((bf16[256,8,128]{2,1,0:T(8,128)(2,1)}), bf16[256,8,128]{2,1,0:T(8,128)(2,1)}, u32[]{:S(2)}, u32[]{:S(2)}) async-start(bf16[256,8,128]{2,1,0:T(8,128)(2,1)} %broadcast_in_dim.529), calls=%async_computation | async-start | bytes 1048576 | tf_op jit(solution)/shard_map/all_to_all | solution.py:120
  47.1 0.7 iota_compare_fusion.9
  47.8 1.2 iota_compare_fusion.7
  49.0 3.5 %bitcast_select_fusion = (bf16[192,2048]{1,0:T(8,128)(2,1)}, bf16[192,2048]{1,0:T(8,128)(2,1)S(1)}, bf16[192,2048]{1,0:T(8,128)(2,1)}) fusion(bf16[1,576,2048]{2,1,0:T(8,128)(2,1)} %param.9, s32[]{:T(128)S(6)} %select_n.313, pred[192]{0:T(512)(128)(4,1)S(1)} %get-tuple-element.135, s32[]{:T(128)S(6)} %select_n.297, pred[192]{0:T(512)(128)(4,1)S(1)} %iota_compare_fusion.9, ...), kind=kLoop, calls=%fused_computation.26 | loop fusion | flops 1179648 | bytes 4719180 | tf_op jit(solution)/shard_map/jit(_where)/select_n | solution.py:151
  52.6 2.2 %collective-permute-start.3 = (bf16[192,2048]{1,0:T(8,128)(2,1)}, bf16[192,2048]{1,0:T(8,128)(2,1)}, u32[]{:S(2)}, u32[]{:S(2)}) collective-permute-start(bf16[192,2048]{1,0:T(8,128)(2,1)} %get-tuple-element.24), channel_id=1, source_target_pairs={{0,252},{4,0},{8,4},{12,8},{16,12},{20,16},{24,20},{28,24},{32,28}... | collective-permute-start | bytes 2359304 | tf_op jit(solution)/shard_map/ppermute | solution.py:19
  58.5 4.0 %dynamic_update_slice.15 = bf16[576,2048]{1,0:T(8,128)(2,1)S(1)} dynamic-update-slice(bf16[576,2048]{1,0:T(8,128)(2,1)S(1)} %broadcast_in_dim.523, bf16[192,2048]{1,0:T(8,128)(2,1)S(1)} %get-tuple-element.25, s32[]{:T(128)S(6)} %select_n.300, s32[]{:T(128)} %constant.62.clone.1) | dynamic-update-slice | bytes 1572868 | tf_op jit(solution)/shard_map/dynamic_update_slice | solution.py:102
  62.6 0.7 fusion.236
  63.2 0.7 fusion.235
  63.9 2.1 %pad_add_fusion.2 = s32[3]{0:T(128)S(1)} fusion(s32[1]{0:T(128)} %get-tuple-element.130, s32[1]{0:T(128)} %get-tuple-element.132, s32[1]{0:T(128)} %bitcast.52), kind=kLoop, calls=%fused_computation.323 | loop fusion | flops 6 | bytes 24 | tf_op jit(solution)/shard_map/stack | solution.py:105
  66.0 0.8 sort.15
  66.9 0.7 fusion.234
  74.2 2.1 select_select_fusion
  76.4 0.7 slice_compare_fusion.31
  77.1 0.7 slice_compare_fusion.61
  77.8 0.7 slice_compare_fusion.62
  78.5 0.7 slice_compare_fusion.29
  83.4 0.7 slice_compare_fusion.30
  84.1 1.4 dynamic-slice_add_fusion.1
  85.6 4.0 %dynamic_update_slice.16 = bf16[576,2048]{1,0:T(8,128)(2,1)S(1)} dynamic-update-slice(bf16[576,2048]{1,0:T(8,128)(2,1)S(1)} %dynamic_update_slice.15, bf16[192,2048]{1,0:T(8,128)(2,1)S(1)} %dynamic-slice_add_fusion.1, s32[]{:T(128)S(6)} %select_n.304, s32[]{:T(128)} %constant.62.clone.1) | dynamic-update-slice | bytes 1572868 | tf_op jit(solution)/shard_map/dynamic_update_slice | solution.py:102
  89.6 1.4 dynamic-slice_add_fusion
  91.1 4.0 %dynamic_update_slice.17 = bf16[576,2048]{1,0:T(8,128)(2,1)S(1)} dynamic-update-slice(bf16[576,2048]{1,0:T(8,128)(2,1)S(1)} %dynamic_update_slice.16, bf16[192,2048]{1,0:T(8,128)(2,1)S(1)} %dynamic-slice_add_fusion, s32[]{:T(128)S(6)} %select_n.311, s32[]{:T(128)} %constant.62.clone.1) | dynamic-update-slice | bytes 1572868 | tf_op jit(solution)/shard_map/dynamic_update_slice | solution.py:102
  96.0 2.2 %shard_map.91 = f32[128,2048]{1,0:T(8,128)} custom-call(bf16[2048,128]{1,0:T(8,128)(2,1)} %bitcast.16.small_ref), custom_call_target="tpu_custom_call" | custom-call | tf_op jit(solution)/shard_map/pallas_call | solution.py:69
  98.2 1.6 fusion.233
  99.8 2.3 %fusion.232 = (f32[1,2048]{1,0:T(1,128)}, f32[1,2048]{1,0:T(1,128)S(1)}, f32[1,2048]{1,0:T(1,128)S(1)}, f32[1,2048]{1,0:T(1,128)S(1)}, f32[1,2048]{1,0:T(1,128)S...) fusion(f32[128,2048]{1,0:T(8,128)} %shard_map.91), kind=kLoop, calls=%fused_computation.407 | loop fusion | bytes 311296 | tf_op jit(solution)/shard_map/slice | solution.py:126
  102.2 52.4 %all-gather.2.cloned.1.call-done = bf16[2048,6144]{1,0:T(8,128)(2,1)} async-done(((bf16[8,6144]{1,0:T(8,128)(2,1)}), bf16[2048,6144]{1,0:T(8,128)(2,1)}) %all-gather.2.cloned.1.call-update) | async-done | bytes 25165840 | tf_op jit(solution)/shard_map/all_gather | solution.py:116
  154.6 10.3 %fusion = f32[384,4096]{1,0:T(8,128)S(1)} fusion(bf16[2048,6144]{1,0:T(8,128)(2,1)} %all-gather.2.cloned.1.call-done, f32[2048]{0:T(1024)S(1)} %bitcast.196, f32[384]{0:T(512)S(1)} %add_rsqrt_fusion.1, f32[384]{0:T(512)S(1)} %broadcast_multiply_fusion.1, bf16[576,2048]{1,0:T(8,128)(2,1)S(1)} %dynamic_update_slice.17), kind=kOutput, calls=%fused_computation | convolution fusion | flops 6446383104 | bytes 24653824 | tf_op jit(solution)/shard_map/dot_general | solution.py:82
  164.9 0.8 fusion.13
  166.2 13.1 %multiply_add_fusion = f32[384,2048]{1,0:T(8,128)} fusion(f32[384,2048]{1,0:T(8,128)S(1)} %fusion.13, f32[2048]{0:T(1024)S(1)} %bitcast.141, f32[2048]{0:T(1024)S(1)} %bitcast.144, f32[2048]{0:T(1024)S(1)} %bitcast.147, f32[2048]{0:T(1024)S(1)} %bitcast.150, f32[2048]{0:T(1024)S(1)} %bitcast.153, f32[2048]{0:T(1024)S(1)} %bitcast.156, ...), kind=kLoop, calls=%fused_computation.20 | loop fusion | flops 49545216 | bytes 6553600 | tf_op jit(solution)/shard_map/add | solution.py:49
  179.7 5.0 %fusion.116 = f32[32,2048]{1,0:T(8,128)S(1)} fusion(s32[]{:T(128)S(6)} %add.543, f32[384,2048]{1,0:T(8,128)S(1)} %fusion.13, s32[]{:T(128)S(6)} %add.542, s32[]{:T(128)S(6)} %add.541, s32[]{:T(128)S(6)} %add.540, s32[]{:T(128)S(6)} %add.539, s32[]{:T(128)S(6)} %add.538, s32[]{:T(128)S(6)} %add.537, s32[]{:T(128)S(6)} %add.536, s32[]{:T(128)S(6)} %add.535, ...), kind=kLoop, calls=%fused_computation.187 | loop fusion | flops 6225920 | bytes 3671168 | tf_op jit(solution)/shard_map/add | solution.py:58
  184.7 1.8 dynamic_update_slice.18
  186.5 4.8 %fusion.119 = f32[32,2048]{1,0:T(8,128)S(1)} fusion(s32[]{:T(128)S(6)} %add.574, f32[384,2048]{1,0:T(8,128)S(1)} %fusion.13, s32[]{:T(128)S(6)} %add.573, s32[]{:T(128)S(6)} %add.572, s32[]{:T(128)S(6)} %add.571, s32[]{:T(128)S(6)} %add.570, s32[]{:T(128)S(6)} %add.569, s32[]{:T(128)S(6)} %add.568, s32[]{:T(128)S(6)} %add.567, s32[]{:T(128)S(6)} %add.566, ...), kind=kLoop, calls=%fused_computation.190 | loop fusion | flops 6225920 | bytes 3671168 | tf_op jit(solution)/shard_map/add | solution.py:58
  191.3 1.8 dynamic_update_slice.19
  193.2 2.3 %reduce_sum.158 = f32[384]{0:T(512)S(1)} reduce(f32[384,2048]{1,0:T(8,128)} %dynamic_update_slice.19, f32[]{:T(128)} %constant.67.clone.1), dimensions={1}, to_apply=%region_16.17 | reduce | flops 786048 | bytes 3147268 | tf_op jit(solution)/shard_map/reduce_sum | solution.py:34
  195.5 0.6 copy-done
  196.5 1.2 multiply_convert_fusion
  198.1 8.0 %fusion.16 = bf16[1,384,2048]{2,1,0:T(8,128)(2,1)} fusion(bf16[384,2048]{1,0:T(8,128)(2,1)S(1)} %multiply_convert_fusion, bf16[2048,6144]{1,0:T(8,128)(2,1)} %all-gather.2.cloned.1.call-done, bf16[576,2048]{1,0:T(8,128)(2,1)S(1)} %copy-done.2), kind=kOutput, calls=%fused_computation.21 | convolution fusion | flops 3223584768 | bytes 13107200 | tf_op jit(solution)/shard_map/dot_general | solution.py:87
  (117 shorter events, 2.4 us)
Async XLA Ops:
  6.5 148.1 %all-gather.2.cloned.1.call-start = ((), (), s32[]{:S(2)}) async-start(), calls=%async_computation.1 | async-start | bytes 25264128 | tf_op jit(solution)/shard_map/all_gather | solution.py:116
  19.5 43.1 %collective-permute-start = (s32[2]{0:T(128)S(1)}, s32[2]{0:T(128)S(1)}, u32[]{:S(2)}, u32[]{:S(2)}) collective-permute-start(s32[2]{0:T(128)S(1)} %get-tuple-element.133), channel_id=1, source_target_pairs={{0,4},{4,8},{8,12},{12,16},{16,20},{20,24},{24,28},{28,32},{32,36}... | collective-permute-start | bytes 32 | tf_op jit(solution)/shard_map/ppermute | solution.py:19
  22.2 41.1 %collective-permute-start.2 = (s32[2]{0:T(128)S(1)}, s32[2]{0:T(128)S(1)}, u32[]{:S(2)}, u32[]{:S(2)}) collective-permute-start(s32[2]{0:T(128)S(1)} %get-tuple-element.134), channel_id=1, source_target_pairs={{0,252},{4,0},{8,4},{12,8},{16,12},{20,16},{24,20},{28,24},{32,28}... | collective-permute-start | bytes 32 | tf_op jit(solution)/shard_map/ppermute | solution.py:19
  25.9 70.1 %all-to-all-start = ((bf16[256,8,128]{2,1,0:T(8,128)(2,1)}), bf16[256,8,128]{2,1,0:T(8,128)(2,1)}, u32[]{:S(2)}, u32[]{:S(2)}) async-start(bf16[256,8,128]{2,1,0:T(8,128)(2,1)} %broadcast_in_dim.529), calls=%async_computation | async-start | bytes 1048576 | tf_op jit(solution)/shard_map/all_to_all | solution.py:120
  52.6 37.1 %collective-permute-start.3 = (bf16[192,2048]{1,0:T(8,128)(2,1)}, bf16[192,2048]{1,0:T(8,128)(2,1)}, u32[]{:S(2)}, u32[]{:S(2)}) collective-permute-start(bf16[192,2048]{1,0:T(8,128)(2,1)} %get-tuple-element.24), channel_id=1, source_target_pairs={{0,252},{4,0},{8,4},{12,8},{16,12},{20,16},{24,20},{28,24},{32,28}... | collective-permute-start | bytes 2359304 | tf_op jit(solution)/shard_map/ppermute | solution.py:19
  54.8 29.3 %collective-permute-start.1 = (bf16[192,2048]{1,0:T(8,128)(2,1)}, bf16[192,2048]{1,0:T(8,128)(2,1)}, u32[]{:S(2)}, u32[]{:S(2)}) collective-permute-start(bf16[192,2048]{1,0:T(8,128)(2,1)} %get-tuple-element.26), channel_id=1, source_target_pairs={{0,4},{4,8},{8,12},{12,16},{16,20},{20,24},{24,28},{28,32},{32,36}... | collective-permute-start | bytes 2359304 | tf_op jit(solution)/shard_map/ppermute | solution.py:19
  95.1 59.5 %copy-start.1 = (bf16[576,2048]{1,0:T(8,128)(2,1)}, bf16[576,2048]{1,0:T(8,128)(2,1)S(1)}, u32[]{:S(2)}) copy-start(bf16[576,2048]{1,0:T(8,128)(2,1)S(1)} %dynamic_update_slice.17) | copy-start | bytes 7077892
  102.1 63.6 %copy-start.3 = (f32[1,2048]{1,0:T(1,128)}, f32[1,2048]{1,0:T(1,128)S(1)}, u32[]{:S(2)}) copy-start(f32[1,2048]{1,0:T(1,128)S(1)} %get-tuple-element.32) | copy-start | bytes 24580
  102.1 63.7 %copy-start.4 = (f32[1,2048]{1,0:T(1,128)}, f32[1,2048]{1,0:T(1,128)S(1)}, u32[]{:S(2)}) copy-start(f32[1,2048]{1,0:T(1,128)S(1)} %get-tuple-element.33) | copy-start | bytes 24580
  102.1 63.7 %copy-start.5 = (f32[1,2048]{1,0:T(1,128)}, f32[1,2048]{1,0:T(1,128)S(1)}, u32[]{:S(2)}) copy-start(f32[1,2048]{1,0:T(1,128)S(1)} %get-tuple-element.34) | copy-start | bytes 24580
  102.1 63.7 %copy-start.6 = (f32[1,2048]{1,0:T(1,128)}, f32[1,2048]{1,0:T(1,128)S(1)}, u32[]{:S(2)}) copy-start(f32[1,2048]{1,0:T(1,128)S(1)} %get-tuple-element.35) | copy-start | bytes 24580
  102.1 63.7 %copy-start.7 = (f32[1,2048]{1,0:T(1,128)}, f32[1,2048]{1,0:T(1,128)S(1)}, u32[]{:S(2)}) copy-start(f32[1,2048]{1,0:T(1,128)S(1)} %get-tuple-element.36) | copy-start | bytes 24580
  102.2 63.7 %copy-start.8 = (f32[1,2048]{1,0:T(1,128)}, f32[1,2048]{1,0:T(1,128)S(1)}, u32[]{:S(2)}) copy-start(f32[1,2048]{1,0:T(1,128)S(1)} %get-tuple-element.37) | copy-start | bytes 24580
  102.2 63.7 %copy-start.9 = (f32[1,2048]{1,0:T(1,128)}, f32[1,2048]{1,0:T(1,128)S(1)}, u32[]{:S(2)}) copy-start(f32[1,2048]{1,0:T(1,128)S(1)} %get-tuple-element.38) | copy-start | bytes 24580
  102.2 63.7 %copy-start.10 = (f32[1,2048]{1,0:T(1,128)}, f32[1,2048]{1,0:T(1,128)S(1)}, u32[]{:S(2)}) copy-start(f32[1,2048]{1,0:T(1,128)S(1)} %get-tuple-element.39) | copy-start | bytes 24580
  102.2 63.7 %copy-start.11 = (f32[1,2048]{1,0:T(1,128)}, f32[1,2048]{1,0:T(1,128)S(1)}, u32[]{:S(2)}) copy-start(f32[1,2048]{1,0:T(1,128)S(1)} %get-tuple-element.40) | copy-start | bytes 24580
  102.2 63.7 %copy-start.12 = (f32[1,2048]{1,0:T(1,128)}, f32[1,2048]{1,0:T(1,128)S(1)}, u32[]{:S(2)}) copy-start(f32[1,2048]{1,0:T(1,128)S(1)} %get-tuple-element.41) | copy-start | bytes 24580
  102.2 63.7 %copy-start.13 = (f32[1,2048]{1,0:T(1,128)}, f32[1,2048]{1,0:T(1,128)S(1)}, u32[]{:S(2)}) copy-start(f32[1,2048]{1,0:T(1,128)S(1)} %get-tuple-element.42) | copy-start | bytes 24580
  102.2 63.7 %copy-start.14 = (f32[1,2048]{1,0:T(1,128)}, f32[1,2048]{1,0:T(1,128)S(1)}, u32[]{:S(2)}) copy-start(f32[1,2048]{1,0:T(1,128)S(1)} %get-tuple-element.43) | copy-start | bytes 24580
  102.2 63.7 %copy-start.15 = (f32[1,2048]{1,0:T(1,128)}, f32[1,2048]{1,0:T(1,128)S(1)}, u32[]{:S(2)}) copy-start(f32[1,2048]{1,0:T(1,128)S(1)} %get-tuple-element.44) | copy-start | bytes 24580
  102.2 63.7 %copy-start.16 = (f32[1,2048]{1,0:T(1,128)}, f32[1,2048]{1,0:T(1,128)S(1)}, u32[]{:S(2)}) copy-start(f32[1,2048]{1,0:T(1,128)S(1)} %get-tuple-element.45) | copy-start | bytes 24580
  165.9 13.5 %copy-start.18 = (pred[32]{0:T(512)(128)(4,1)S(1)}, pred[32]{0:T(512)(128)(4,1)}, u32[]{:S(2)}) copy-start(pred[32]{0:T(512)(128)(4,1)} %get-tuple-element.114) | copy-start | bytes 100
  165.9 13.5 %copy-start.19 = (pred[32]{0:T(512)(128)(4,1)S(1)}, pred[32]{0:T(512)(128)(4,1)}, u32[]{:S(2)}) copy-start(pred[32]{0:T(512)(128)(4,1)} %get-tuple-element.115) | copy-start | bytes 100
  165.9 13.4 %copy-start.20 = (pred[32]{0:T(512)(128)(4,1)S(1)}, pred[32]{0:T(512)(128)(4,1)}, u32[]{:S(2)}) copy-start(pred[32]{0:T(512)(128)(4,1)} %get-tuple-element.116) | copy-start | bytes 100
  165.9 13.4 %copy-start.21 = (pred[32]{0:T(512)(128)(4,1)S(1)}, pred[32]{0:T(512)(128)(4,1)}, u32[]{:S(2)}) copy-start(pred[32]{0:T(512)(128)(4,1)} %get-tuple-element.117) | copy-start | bytes 100
  165.9 13.4 %copy-start.22 = (pred[32]{0:T(512)(128)(4,1)S(1)}, pred[32]{0:T(512)(128)(4,1)}, u32[]{:S(2)}) copy-start(pred[32]{0:T(512)(128)(4,1)} %get-tuple-element.118) | copy-start | bytes 100
  166.0 13.4 %copy-start.23 = (pred[32]{0:T(512)(128)(4,1)S(1)}, pred[32]{0:T(512)(128)(4,1)}, u32[]{:S(2)}) copy-start(pred[32]{0:T(512)(128)(4,1)} %get-tuple-element.119) | copy-start | bytes 100
  166.0 13.4 %copy-start.24 = (pred[32]{0:T(512)(128)(4,1)S(1)}, pred[32]{0:T(512)(128)(4,1)}, u32[]{:S(2)}) copy-start(pred[32]{0:T(512)(128)(4,1)} %get-tuple-element.120) | copy-start | bytes 100
  166.0 13.4 %copy-start.25 = (pred[32]{0:T(512)(128)(4,1)S(1)}, pred[32]{0:T(512)(128)(4,1)}, u32[]{:S(2)}) copy-start(pred[32]{0:T(512)(128)(4,1)} %get-tuple-element.121) | copy-start | bytes 100
  166.0 13.4 %copy-start.26 = (pred[32]{0:T(512)(128)(4,1)S(1)}, pred[32]{0:T(512)(128)(4,1)}, u32[]{:S(2)}) copy-start(pred[32]{0:T(512)(128)(4,1)} %get-tuple-element.122) | copy-start | bytes 100
  166.0 13.4 %copy-start.27 = (pred[32]{0:T(512)(128)(4,1)S(1)}, pred[32]{0:T(512)(128)(4,1)}, u32[]{:S(2)}) copy-start(pred[32]{0:T(512)(128)(4,1)} %get-tuple-element.123) | copy-start | bytes 100
  166.0 13.4 %copy-start.28 = (pred[32]{0:T(512)(128)(4,1)S(1)}, pred[32]{0:T(512)(128)(4,1)}, u32[]{:S(2)}) copy-start(pred[32]{0:T(512)(128)(4,1)} %get-tuple-element.124) | copy-start | bytes 100
  166.0 13.4 %copy-start.29 = (pred[32]{0:T(512)(128)(4,1)S(1)}, pred[32]{0:T(512)(128)(4,1)}, u32[]{:S(2)}) copy-start(pred[32]{0:T(512)(128)(4,1)} %get-tuple-element.125) | copy-start | bytes 100
  166.0 13.4 %copy-start.30 = (pred[32]{0:T(512)(128)(4,1)S(1)}, pred[32]{0:T(512)(128)(4,1)}, u32[]{:S(2)}) copy-start(pred[32]{0:T(512)(128)(4,1)} %get-tuple-element.126) | copy-start | bytes 100
  166.0 13.4 %copy-start.31 = (pred[32]{0:T(512)(128)(4,1)S(1)}, pred[32]{0:T(512)(128)(4,1)}, u32[]{:S(2)}) copy-start(pred[32]{0:T(512)(128)(4,1)} %get-tuple-element.61) | copy-start | bytes 100
  166.0 13.4 %copy-start.32 = (pred[32]{0:T(512)(128)(4,1)S(1)}, pred[32]{0:T(512)(128)(4,1)}, u32[]{:S(2)}) copy-start(pred[32]{0:T(512)(128)(4,1)} %get-tuple-element.96) | copy-start | bytes 100
  166.1 13.4 %copy-start.33 = (pred[32]{0:T(512)(128)(4,1)S(1)}, pred[32]{0:T(512)(128)(4,1)}, u32[]{:S(2)}) copy-start(pred[32]{0:T(512)(128)(4,1)} %get-tuple-element.97) | copy-start | bytes 100
  166.1 13.4 %copy-start.34 = (pred[32]{0:T(512)(128)(4,1)S(1)}, pred[32]{0:T(512)(128)(4,1)}, u32[]{:S(2)}) copy-start(pred[32]{0:T(512)(128)(4,1)} %get-tuple-element.98) | copy-start | bytes 100
  166.1 13.4 %copy-start.35 = (pred[32]{0:T(512)(128)(4,1)S(1)}, pred[32]{0:T(512)(128)(4,1)}, u32[]{:S(2)}) copy-start(pred[32]{0:T(512)(128)(4,1)} %get-tuple-element.99) | copy-start | bytes 100
  166.1 13.4 %copy-start.36 = (pred[32]{0:T(512)(128)(4,1)S(1)}, pred[32]{0:T(512)(128)(4,1)}, u32[]{:S(2)}) copy-start(pred[32]{0:T(512)(128)(4,1)} %get-tuple-element.100) | copy-start | bytes 100
  166.1 13.4 %copy-start.37 = (pred[32]{0:T(512)(128)(4,1)S(1)}, pred[32]{0:T(512)(128)(4,1)}, u32[]{:S(2)}) copy-start(pred[32]{0:T(512)(128)(4,1)} %get-tuple-element.101) | copy-start | bytes 100
  166.1 13.4 %copy-start.38 = (pred[32]{0:T(512)(128)(4,1)S(1)}, pred[32]{0:T(512)(128)(4,1)}, u32[]{:S(2)}) copy-start(pred[32]{0:T(512)(128)(4,1)} %get-tuple-element.102) | copy-start | bytes 100
  166.1 13.4 %copy-start.39 = (pred[32]{0:T(512)(128)(4,1)S(1)}, pred[32]{0:T(512)(128)(4,1)}, u32[]{:S(2)}) copy-start(pred[32]{0:T(512)(128)(4,1)} %get-tuple-element.103) | copy-start | bytes 100
  166.1 13.4 %copy-start.40 = (pred[32]{0:T(512)(128)(4,1)S(1)}, pred[32]{0:T(512)(128)(4,1)}, u32[]{:S(2)}) copy-start(pred[32]{0:T(512)(128)(4,1)} %get-tuple-element.104) | copy-start | bytes 100
  166.1 13.4 %copy-start.41 = (pred[32]{0:T(512)(128)(4,1)S(1)}, pred[32]{0:T(512)(128)(4,1)}, u32[]{:S(2)}) copy-start(pred[32]{0:T(512)(128)(4,1)} %get-tuple-element.105) | copy-start | bytes 100
  166.1 13.4 %copy-start.42 = (pred[32]{0:T(512)(128)(4,1)S(1)}, pred[32]{0:T(512)(128)(4,1)}, u32[]{:S(2)}) copy-start(pred[32]{0:T(512)(128)(4,1)} %get-tuple-element.106) | copy-start | bytes 100
  166.2 13.4 %copy-start.43 = (pred[32]{0:T(512)(128)(4,1)S(1)}, pred[32]{0:T(512)(128)(4,1)}, u32[]{:S(2)}) copy-start(pred[32]{0:T(512)(128)(4,1)} %get-tuple-element.107) | copy-start | bytes 100
  166.2 13.4 %copy-start.44 = (pred[32]{0:T(512)(128)(4,1)S(1)}, pred[32]{0:T(512)(128)(4,1)}, u32[]{:S(2)}) copy-start(pred[32]{0:T(512)(128)(4,1)} %get-tuple-element.108) | copy-start | bytes 100
  (8 other events, 75.0 us)
Sparse Core Ops, SparseCore 0:
  11.2 143.3 all-gather.1

commit v7 on v6

--- a/solution.py
+++ b/solution.py
@@ -47,16 +47,25 @@
     depthwise = jnp.zeros_like(gated_rows)
     for column in range(KERNEL):
         depthwise = depthwise + padded[column : column + row_count] * taps[column : column + 1]
+    position = jnp.arange(row_count, dtype=jnp.int32)
     for bound in bounds:
         start = bound - margin
-        window = lax.dynamic_slice_in_dim(padded, start, 2 * KERNEL, 0)
-        window_labels = lax.dynamic_slice_in_dim(labels, start, 2 * KERNEL, 0)
-        own = lax.dynamic_slice_in_dim(segment, start, KERNEL, 0)
+        window, window_labels, own = lax.optimization_barrier(
+            (
+                lax.dynamic_slice_in_dim(padded, start, 2 * KERNEL, 0),
+                lax.dynamic_slice_in_dim(labels, start, 2 * KERNEL, 0),
+                lax.dynamic_slice_in_dim(segment, start, KERNEL, 0),
+            )
+        )
         exact = jnp.zeros((KERNEL, gated_rows.shape[1]), gated_rows.dtype)
         for column in range(KERNEL):
             inside = (window_labels[column : column + KERNEL] == own)[:, None]
             exact = exact + jnp.where(inside, window[column : column + KERNEL], 0.0) * taps[column : column + 1]
-        depthwise = lax.dynamic_update_slice_in_dim(depthwise, exact, start, 0)
+        relative = position - start
+        placement = (relative[:, None] == jnp.arange(KERNEL, dtype=jnp.int32)[None, :]).astype(jnp.float32)
+        placed = jnp.dot(placement, exact, precision=lax.Precision.HIGHEST)
+        covered = ((relative >= 0) & (relative < KERNEL))[:, None]
+        depthwise = jnp.where(covered, placed, depthwise)
     return depthwise
 
 
@@ -83,7 +92,7 @@
     gated_rows = projected[:, :widths] * jax.nn.sigmoid(projected[:, widths:])
     depthwise = depth_pass(gated_rows, segment, taps, bounds)
     normed_post = layer_norm(depthwise, post_gain)
-    active = lax.optimization_barrier((normed_post * jax.nn.sigmoid(normed_post)).astype(jnp.bfloat16))
+    active = (normed_post * jax.nn.sigmoid(normed_post)).astype(jnp.bfloat16)
     return (source + jnp.dot(active, weight_out, preferred_element_type=jnp.float32)).astype(
         jnp.bfloat16
     )

time: 214 us -> 243 us (1.14)
  matrix products: 18.3 us -> 76.3 us
  other arithmetic: 59.1 us -> 30.8 us
  local copies, waits for them, and re-layouts: 25.6 us -> 20.6 us
  waiting for transfers between devices: 52.4 us -> 57.3 us
    dot_general x0 -> x2, matrix products: none -> 57.8 us  [depth_pass(): placed = jnp.dot(placement, exact, precision=lax.Precision.HIGHEST)]
    add x3 -> x0, other arithmetic: 23 us -> none  [the longest x1 13.1 us: depth_pass(): depthwise + padded[column:column + row_count] * taps[column:column + 1]]
    all_gather x1, waiting for transfers between devices: 52.4 us -> 57.3 us  [shards(): gathered = lax.all_gather(both, ('dp', 'group'), axis=0, tiled=True)]
    dynamic_update_slice x2 -> x0, local copies, waits for them, and re-layouts: 3.67 us -> none  [depth_pass(): depthwise = lax.dynamic_update_slice_in_dim(depthwise, exact, start, 0)]
    eq x5 -> x4, other arithmetic: 3.55 us -> 0.36 us  [depth_pass(): inside = (window_labels[column:column + KERNEL] == own)[:, None]]
  transfers between devices with their start and end apart: 6 -> 6, of which waited for: 1 -> 1; matrix products, arithmetic and copies ran while one was open for 24% -> 19% of each run, Pallas kernels for 1% -> 1%
where the time goes in v7:
time: 243 us; the launch traced here: 242 us
  matrix products  76.3 us (31%)
  waiting for transfers between devices  57.3 us (24%)
  between operations  32.3 us (13%)
  other arithmetic  30.8 us (13%)
  starting transfers between devices  22 us (9%)
  local copies, waits for them, and re-layouts  20.6 us (8%)
    dot_general x2, matrix products, depth_pass(): placed = jnp.dot(placement, exact, precision=lax.Precision.HIGHEST)  57.8 us
    all_gather x1, waiting for transfers between devices, shards(): gathered = lax.all_gather(both, ('dp', 'group'), axis=0, tiled=True)  57.3 us
    all_to_all x1, starting transfers between devices, shards(): spread = lax.all_to_all(copies, ('dp', 'group'), 0, 0, tiled=True)  16.5 us
    dynamic_update_slice x3, local copies, waits for them, and re-layouts, relocate(): lax.dynamic_update_slice_in_dim(received, current + frame_rows, meta_data...  12.1 us
    dot_general x1, matrix products, conv_module(): projected = jnp.dot(normed, weight_in, preferred_element_type=jnp.float32)  10.3 us
    dot_general x1, matrix products, conv_module(): jnp.dot(active, weight_out, preferred_element_type=jnp.float32)  8.15 us
    reduce_sum x2, other arithmetic, pick_entry(): return jnp.sum(jnp.where(slot_ids == which, values, 0))  6.47 us
    ppermute x4, starting transfers between devices, shifted(): lax.ppermute(array, axis, [(i, (i + by) % peers) for i in range(peers)])  5.49 us
  transfers between devices with their start and end apart: 6, of which 1 were waited for; matrix products, arithmetic and copies ran while one was open for 19% of the time, Pallas kernels for 1%

profile of v7, /device:TPU:1, one launch (start us, length us, event | category | flops | bytes accessed | tf_op | source)
XLA Modules:
  0.0 241.5 jit_solution(13037861059873114399)
XLA Ops:
  6.5 1.5 pad_maximum_fusion
  8.1 0.8 reduce-window.9
  8.9 1.4 fusion.452
  10.2 3.2 %fusion.456 = (s32[]{:T(128)}, s32[]{:T(128)}, s32[]{:T(128)}) fusion(s32[1,3]{1,0:T(1,128)} %param.12, s32[]{:T(128)} %get-tuple-element.29, s32[]{:T(128)} %get-tuple-element.31, s32[]{:T(128)} %get-tuple-element.30), kind=kLoop, calls=%fused_computation.516 | loop fusion | flops 24 | bytes 36 | tf_op jit(solution)/shard_map/reduce_sum | solution.py:148
  13.5 3.3 %select_reduce_fusion = (s32[]{:T(128)}, s32[]{:T(128)}, s32[]{:T(128)}, s32[]{:T(128)}, s32[]{:T(128)}, /*index=5*/s32[]{:T(128)}) fusion(s32[]{:T(128)} %get-tuple-element.30, s32[1,3]{1,0:T(1,128)} %param.10, s32[3,1]{0,1:T(1,128)S(1)} %reduce-window.9, s32[]{:T(128)} %get-tuple-element.31, s32[]{:T(128)} %get-tuple-element.29), kind=kLoop, calls=%fused_computation.590 | loop fusion | flops 42 | bytes 60 | tf_op jit(solution)/shard_map/reduce_sum | solution.py:148
  16.7 1.4 pad_add_fusion.1
  18.1 3.3 %collective-permute-start.2 = (s32[2]{0:T(128)S(1)}, s32[2]{0:T(128)S(1)}, u32[]{:S(2)}, u32[]{:S(2)}) collective-permute-start(s32[2]{0:T(128)S(1)} %pad_add_fusion.1), channel_id=1, source_target_pairs={{0,252},{4,0},{8,4},{12,8},{16,12},{20,16},{24,20},{28,24},{32,28}... | collective-permute-start | bytes 32 | tf_op jit(solution)/shard_map/ppermute | solution.py:19
  21.3 1.3 pad_add_fusion
  22.6 0.7 copy.10
  23.4 0.7 copy.11
  24.1 0.8 fusion.448
  24.9 0.9 broadcast_in_dim.546
  25.8 16.5 %all-to-all-start = ((bf16[256,8,128]{2,1,0:T(8,128)(2,1)}), bf16[256,8,128]{2,1,0:T(8,128)(2,1)}, u32[]{:S(2)}, u32[]{:S(2)}) async-start(bf16[256,8,128]{2,1,0:T(8,128)(2,1)} %broadcast_in_dim.546), calls=%async_computation | async-start | bytes 1048576 | tf_op jit(solution)/shard_map/all_to_all | solution.py:129
  47.7 0.6 iota_compare_fusion.13
  48.4 1.2 iota_compare_fusion.11
  49.6 3.5 %bitcast_select_fusion = (bf16[192,2048]{1,0:T(8,128)(2,1)}, bf16[192,2048]{1,0:T(8,128)(2,1)S(1)}, bf16[192,2048]{1,0:T(8,128)(2,1)}) fusion(bf16[1,576,2048]{2,1,0:T(8,128)(2,1)} %param.9, s32[]{:T(128)S(6)} %select_n.318, pred[192]{0:T(512)(128)(4,1)S(1)} %get-tuple-element.149, s32[]{:T(128)S(6)} %select_n.302, ...), kind=kLoop, calls=%fused_computation.76 | loop fusion | flops 1179648 | bytes 4719180 | tf_op jit(solution)/shard_map/jit(_where)/select_n | solution.py:160
  53.1 2.2 collective-permute-start.3
  58.2 0.3 broadcast_in_dim.539
  58.5 4.0 %dynamic_update_slice.9 = bf16[576,2048]{1,0:T(8,128)(2,1)S(1)} dynamic-update-slice(bf16[576,2048]{1,0:T(8,128)(2,1)S(1)} %broadcast_in_dim.539, bf16[192,2048]{1,0:T(8,128)(2,1)S(1)} %get-tuple-element.35, s32[]{:T(128)S(6)} %select_n.305, s32[]{:T(128)} %constant.63.clone.1) | dynamic-update-slice | bytes 1572868 | tf_op jit(solution)/shard_map/dynamic_update_slice | solution.py:111
  62.6 0.6 fusion.469
  63.2 0.6 fusion.470
  63.8 1.9 pad_add_fusion.2
  68.3 0.8 sort.15
  69.0 0.7 fusion.468
  77.6 1.8 select_select_fusion.1
  79.5 0.1 pad_dynamic-slice_fusion.2
  79.6 1.4 dynamic-slice_add_fusion.1
  81.0 4.0 %dynamic_update_slice.10 = bf16[576,2048]{1,0:T(8,128)(2,1)S(1)} dynamic-update-slice(bf16[576,2048]{1,0:T(8,128)(2,1)S(1)} %dynamic_update_slice.9, bf16[192,2048]{1,0:T(8,128)(2,1)S(1)} %dynamic-slice_add_fusion.1, s32[]{:T(128)S(6)} %select_n.309, s32[]{:T(128)} %constant.63.clone.1) | dynamic-update-slice | bytes 1572868 | tf_op jit(solution)/shard_map/dynamic_update_slice | solution.py:111
  85.1 1.4 dynamic-slice_add_fusion
  86.5 4.0 %dynamic_update_slice.11 = bf16[576,2048]{1,0:T(8,128)(2,1)S(1)} dynamic-update-slice(bf16[576,2048]{1,0:T(8,128)(2,1)S(1)} %dynamic_update_slice.10, bf16[192,2048]{1,0:T(8,128)(2,1)S(1)} %dynamic-slice_add_fusion, s32[]{:T(128)S(6)} %select_n.316, s32[]{:T(128)} %constant.63.clone.1) | dynamic-update-slice | bytes 1572868 | tf_op jit(solution)/shard_map/dynamic_update_slice | solution.py:111
  90.5 0.3 convert_reduce_fusion
  90.8 0.6 fusion.6
  91.4 2.2 shard_map.91
  93.6 1.6 fusion.466
  95.2 1.7 fusion.465
  96.9 57.3 %all-gather.2.cloned.1.call-done = bf16[2048,6144]{1,0:T(8,128)(2,1)} async-done(((bf16[8,6144]{1,0:T(8,128)(2,1)}), bf16[2048,6144]{1,0:T(8,128)(2,1)}) %all-gather.2.cloned.1.call-update) | async-done | bytes 25165840 | tf_op jit(solution)/shard_map/all_gather | solution.py:125
  154.2 10.3 %fusion = f32[384,4096]{1,0:T(8,128)S(1)} fusion(bf16[2048,6144]{1,0:T(8,128)(2,1)} %all-gather.2.cloned.1.call-done, f32[2048]{0:T(1024)S(1)} %bitcast.163, f32[384]{0:T(512)S(1)} %add_rsqrt_fusion.1, f32[384]{0:T(512)S(1)} %broadcast_multiply_fusion.1, bf16[576,2048]{1,0:T(8,128)(2,1)S(1)} %dynamic_update_slice.11), kind=kOutput, calls=%fused_computation | convolution fusion | flops 6446383104 | bytes 24653824 | tf_op jit(solution)/shard_map/dot_general | solution.py:91
  164.5 0.8 fusion.13
  165.4 0.2 pad_dynamic-slice_fusion
  165.5 0.1 slice_compare_fusion.30
  165.6 0.1 slice_compare_fusion.31
  165.7 0.1 slice_compare_fusion.62
  165.8 0.1 slice_compare_fusion.63
  165.9 4.8 %fusion.184 = f32[384,2048]{1,0:T(8,128)} fusion(f32[64,2048]{1,0:T(8,128)S(1)} %get-tuple-element.16, f32[2048]{0:T(1024)S(1)} %bitcast.127, f32[2048]{0:T(1024)S(1)} %bitcast.129, f32[2048]{0:T(1024)S(1)} %bitcast.131, f32[2048]{0:T(1024)S(1)} %bitcast.133, f32[2048]{0:T(1024)S(1)} %bitcast.135, f32[2048]{0:T(1024)S(1)} %bitcast.137, ...), kind=kOutput, calls=%fused_computation.208 | convolution fusion | flops 308228096 | bytes 11814912 | tf_op jit(solution)/shard_map/dot_general | solution.py:66
  170.7 53.0 %fusion.471 = (f32[384]{0:T(512)S(1)}, f32[384,2048]{1,0:T(8,128)}) fusion(f32[384,2048]{1,0:T(8,128)} %fusion.184, f32[2048]{0:T(1024)S(1)} %bitcast.128, f32[2048]{0:T(1024)S(1)} %bitcast.130, f32[2048]{0:T(1024)S(1)} %bitcast.132, f32[2048]{0:T(1024)S(1)} %bitcast.134, f32[2048]{0:T(1024)S(1)} %bitcast.136, f32[2048]{0:T(1024)S(1)} %bitcast.138, ...), kind=kOutput, calls=%fused_computation.605 | convolution fusion | flops 360132224 | bytes 18371072 | tf_op jit(solution)/shard_map/dot_general | solution.py:66
  223.7 2.5 %multiply_reduce_fusion = f32[384]{0:T(512)S(1)} fusion(f32[384,2048]{1,0:T(8,128)} %get-tuple-element.146, f32[384]{0:T(512)S(1)} %broadcast_multiply_fusion), kind=kLoop, calls=%fused_computation.19 | loop fusion | flops 2358912 | bytes 3148800 | tf_op jit(solution)/shard_map/reduce_sum | solution.py:35
  226.2 0.3 copy-done.1
  226.5 8.2 %fusion.45 = bf16[1,384,2048]{2,1,0:T(8,128)(2,1)} fusion(bf16[2048,6144]{1,0:T(8,128)(2,1)} %all-gather.2.cloned.1.call-done, f32[384,2048]{1,0:T(8,128)S(1)} %copy-done.1, f32[2048]{0:T(1024)S(1)} %bitcast.98, f32[384]{0:T(512)S(1)} %add_rsqrt_fusion, f32[384]{0:T(512)S(1)} %broadcast_multiply_fusion, bf16[576,2048]{1,0:T(8,128)(2,1)S(1)} %dynamic_update_slice.11), kind=kOutput, calls=%fused_computation.67 | convolution fusion | flops 3229876224 | bytes 14691328 | tf_op jit(solution)/shard_map/dot_general | solution.py:96
  (21 shorter events, 0.2 us)
Async XLA Ops:
  6.5 147.7 %all-gather.2.cloned.1.call-start = ((), (), s32[]{:S(2)}) async-start(), calls=%async_computation.1 | async-start | bytes 25264128 | tf_op jit(solution)/shard_map/all_gather | solution.py:125
  18.1 44.5 %collective-permute-start.2 = (s32[2]{0:T(128)S(1)}, s32[2]{0:T(128)S(1)}, u32[]{:S(2)}, u32[]{:S(2)}) collective-permute-start(s32[2]{0:T(128)S(1)} %pad_add_fusion.1), channel_id=1, source_target_pairs={{0,252},{4,0},{8,4},{12,8},{16,12},{20,16},{24,20},{28,24},{32,28}... | collective-permute-start | bytes 32 | tf_op jit(solution)/shard_map/ppermute | solution.py:19
  22.6 40.6 %collective-permute-start = (s32[2]{0:T(128)S(1)}, s32[2]{0:T(128)S(1)}, u32[]{:S(2)}, u32[]{:S(2)}) collective-permute-start(s32[2]{0:T(128)S(1)} %pad_add_fusion), channel_id=1, source_target_pairs={{0,4},{4,8},{8,12},{12,16},{16,20},{20,24},{24,28},{28,32},{32,36}... | collective-permute-start | bytes 32 | tf_op jit(solution)/shard_map/ppermute | solution.py:19
  25.8 65.7 %all-to-all-start = ((bf16[256,8,128]{2,1,0:T(8,128)(2,1)}), bf16[256,8,128]{2,1,0:T(8,128)(2,1)}, u32[]{:S(2)}, u32[]{:S(2)}) async-start(bf16[256,8,128]{2,1,0:T(8,128)(2,1)} %broadcast_in_dim.546), calls=%async_computation | async-start | bytes 1048576 | tf_op jit(solution)/shard_map/all_to_all | solution.py:129
  53.1 31.9 %collective-permute-start.3 = (bf16[192,2048]{1,0:T(8,128)(2,1)}, bf16[192,2048]{1,0:T(8,128)(2,1)}, u32[]{:S(2)}, u32[]{:S(2)}) collective-permute-start(bf16[192,2048]{1,0:T(8,128)(2,1)} %get-tuple-element.34), channel_id=1, source_target_pairs={{0,252},{4,0},{8,4},{12,8},{16,12},{20,16},{24,20},{28,24},{32,28}... | collective-permute-start | bytes 2359304 | tf_op jit(solution)/shard_map/ppermute | solution.py:19
  55.4 24.2 %collective-permute-start.1 = (bf16[192,2048]{1,0:T(8,128)(2,1)}, bf16[192,2048]{1,0:T(8,128)(2,1)}, u32[]{:S(2)}, u32[]{:S(2)}) collective-permute-start(bf16[192,2048]{1,0:T(8,128)(2,1)} %get-tuple-element.36), channel_id=1, source_target_pairs={{0,4},{4,8},{8,12},{12,16},{16,20},{20,24},{24,28},{28,32},{32,36}... | collective-permute-start | bytes 2359304 | tf_op jit(solution)/shard_map/ppermute | solution.py:19
  165.4 5.3 %copy-start = (f32[384,2048]{1,0:T(8,128)}, f32[384,2048]{1,0:T(8,128)S(1)}, u32[]{:S(2)}) copy-start(f32[384,2048]{1,0:T(8,128)S(1)} %fusion.13) | copy-start | bytes 9437188
  223.7 2.8 %copy-start.1 = (f32[384,2048]{1,0:T(8,128)S(1)}, f32[384,2048]{1,0:T(8,128)}, u32[]{:S(2)}) copy-start(f32[384,2048]{1,0:T(8,128)} %get-tuple-element.146) | copy-start | bytes 9437188
Sparse Core Ops, SparseCore 0:
  11.2 142.9 all-gather.1

commit v8 on v5

--- a/solution.py
+++ b/solution.py
@@ -103,7 +103,9 @@
     small = jnp.concatenate([norm_gain[:, None], post_gain[:, None], depth_kernel], axis=1)
     small = jnp.pad(small, ((0, 0), (0, SMALL_WIDTH - small.shape[1])))
     both = jnp.concatenate([weight_in, weight_out], axis=1)
-    gathered = lax.all_gather(both, ("dp", "group"), axis=0, tiled=True)
+    gathered = lax.all_gather(
+        lax.all_gather(both, "group", axis=0, tiled=True), "dp", axis=0, tiled=True
+    )
     columns = weight_in.shape[1] + weight_out.shape[1]
     peers = lax.axis_size(("dp", "group"))
     copies = jnp.broadcast_to(small[None], (peers,) + small.shape)

time: 203 us -> 201 us (level)
  waiting for transfers between devices: 63.7 us -> 50.1 us
  blocking collectives: 0 us -> 12.3 us
  other arithmetic: 45.8 us -> 43.7 us
    all_gather x1, waiting for transfers between devices: 63.6 us -> 50 us  [shards(): lax.all_gather(lax.all_gather(both, 'group', axis=0, tiled=True), 'dp', a...]
    all_gather x0 -> x1, blocking collectives: none -> 12.3 us  [shards(): lax.all_gather(both, 'group', axis=0, tiled=True)]
where the time goes in v8:
time: 201 us; the launch traced here: 200 us
  waiting for transfers between devices  50.1 us (25%)
  other arithmetic  43.7 us (22%)
  between operations  28.6 us (14%)
  starting transfers between devices  25.1 us (12%)
  local copies, waits for them, and re-layouts  19.6 us (10%)
  matrix products  18.6 us (9%)
  blocking collectives  12.3 us (6%)
  Pallas kernels  2.23 us (1%)
    all_gather x1, waiting for transfers between devices, shards(): lax.all_gather(lax.all_gather(both, 'group', axis=0, tiled=True), 'dp', a...  50 us
    reduce_sum x2, other arithmetic, layer_norm(): center = values - jnp.mean(values, axis=-1, keepdims=True)  20 us
    all_to_all x1, starting transfers between devices, shards(): spread = lax.all_to_all(copies, ('dp', 'group'), 0, 0, tiled=True)  17.8 us
    all_gather x1, blocking collectives, shards(): lax.all_gather(both, 'group', axis=0, tiled=True)  12.3 us
    dynamic_update_slice x3, local copies, waits for them, and re-layouts, relocate(): lax.dynamic_update_slice_in_dim(received, current + frame_rows, meta_data...  12.1 us
    dot_general x1, matrix products, conv_module(): projected = jnp.dot(normed, weight_in, preferred_element_type=jnp.float32)  10.3 us
    dot_general x1, matrix products, conv_module(): jnp.dot(active, weight_out, preferred_element_type=jnp.float32)  8.28 us
    ppermute x4, starting transfers between devices, shifted(): lax.ppermute(array, axis, [(i, (i + by) % peers) for i in range(peers)])  7.31 us
  transfers between devices with their start and end apart: 6, of which 1 were waited for; matrix products, arithmetic and copies ran while one was open for 21% of the time, Pallas kernels for 1%

profile of v8, /device:TPU:1, one launch (start us, length us, event | category | flops | bytes accessed | tf_op | source)
XLA Modules:
  0.0 200.2 jit_solution(2845592535635476647)
XLA Ops:
  6.5 1.0 pad_maximum_fusion
  7.6 12.3 %all_gather.6 = bf16[32,6144]{1,0:T(8,128)(2,1)} all-gather(bf16[8,6144]{1,0:T(8,128)(2,1)S(1)} %pad_maximum_fusion), channel_id=1, replica_groups=mesh['dp'=64,'group'=4] {'group'}, dimensions={0}, use_global_device_ids=true | all-gather | bytes 491520 | tf_op jit(solution)/shard_map/all_gather | solution.py:107
  19.9 0.0 all-gather.2.cloned.1.call-update
  19.9 0.7 copy.11
  20.6 0.7 copy.10
  21.4 0.8 fusion.76
  22.1 0.9 broadcast_in_dim.308
  23.0 17.8 %all-to-all-start = ((bf16[256,8,128]{2,1,0:T(8,128)(2,1)}), bf16[256,8,128]{2,1,0:T(8,128)(2,1)}, u32[]{:S(2)}, u32[]{:S(2)}) async-start(bf16[256,8,128]{2,1,0:T(8,128)(2,1)} %broadcast_in_dim.308), calls=%async_computation | async-start | bytes 1048576 | tf_op jit(solution)/shard_map/all_to_all | solution.py:112
  40.8 0.8 reduce-window.9
  41.6 1.3 fusion.82
  43.0 3.1 %fusion.86 = (s32[]{:T(128)}, s32[]{:T(128)}, s32[]{:T(128)}) fusion(s32[1,3]{1,0:T(1,128)} %param.12, s32[]{:T(128)} %get-tuple-element.14, s32[]{:T(128)} %get-tuple-element.15, s32[]{:T(128)} %get-tuple-element.16), kind=kLoop, calls=%fused_computation.166 | loop fusion | flops 24 | bytes 36 | tf_op jit(solution)/shard_map/reduce_sum | solution.py:131
  46.1 3.2 %select_reduce_fusion = (s32[]{:T(128)}, s32[]{:T(128)}, s32[]{:T(128)}, s32[]{:T(128)}, s32[]{:T(128)}, /*index=5*/s32[]{:T(128)}) fusion(s32[]{:T(128)} %get-tuple-element.14, s32[1,3]{1,0:T(1,128)} %param.10, s32[3,1]{0,1:T(1,128)S(1)} %reduce-window.9, s32[]{:T(128)} %get-tuple-element.15, s32[]{:T(128)} %get-tuple-element.16), kind=kLoop, calls=%fused_computation.174 | loop fusion | flops 42 | bytes 60 | tf_op jit(solution)/shard_map/reduce_sum | solution.py:131
  49.4 2.5 %pad_add_fusion = (s32[2]{0:T(128)S(1)}, s32[2]{0:T(128)S(1)}) fusion(s32[1]{0:T(128)} %bitcast.7, s32[1]{0:T(128)} %bitcast.6, s32[1]{0:T(128)} %bitcast.11, s32[1]{0:T(128)} %bitcast.10), kind=kLoop, calls=%fused_computation.159 | loop fusion | flops 4 | bytes 32 | tf_op jit(solution)/shard_map/stack | solution.py:144
  51.9 1.7 collective-permute-start
  53.5 0.7 collective-permute-start.2
  59.8 0.6 iota_compare_fusion.9
  60.4 1.2 iota_compare_fusion.7
  61.7 1.9 bitcast_select_fusion
  63.6 1.1 collective-permute-start.1
  64.7 3.9 %collective-permute-start.3 = (bf16[192,2048]{1,0:T(8,128)(2,1)}, bf16[192,2048]{1,0:T(8,128)(2,1)}, u32[]{:S(2)}, u32[]{:S(2)}) collective-permute-start(bf16[192,2048]{1,0:T(8,128)(2,1)} %get-tuple-element.19), channel_id=1, source_target_pairs={{0,252},{4,0},{8,4},{12,8},{16,12},{20,16},{24,20},{28,24},{32,28}... | collective-permute-start | bytes 2359304 | tf_op jit(solution)/shard_map/ppermute | solution.py:19
  71.4 0.3 broadcast_in_dim.297
  71.7 4.0 %dynamic_update_slice.9 = bf16[576,2048]{1,0:T(8,128)(2,1)S(1)} dynamic-update-slice(bf16[576,2048]{1,0:T(8,128)(2,1)S(1)} %broadcast_in_dim.297, bf16[192,2048]{1,0:T(8,128)(2,1)S(1)} %get-tuple-element.20, s32[]{:T(128)S(6)} %select_n.186, s32[]{:T(128)} %constant.48.clone.1) | dynamic-update-slice | bytes 1572868 | tf_op jit(solution)/shard_map/dynamic_update_slice | solution.py:93
  75.7 0.0 collective-permute-done
  75.7 0.6 fusion.95
  77.7 0.0 collective-permute-done.2
  77.7 0.7 fusion.94
  79.7 1.9 select_select_fusion
  81.6 0.1 slice_compare_fusion.30
  81.7 0.1 slice_compare_fusion.29
  81.7 0.1 slice_compare_fusion.27
  85.8 0.1 slice_compare_fusion.28
  85.9 1.4 dynamic-slice_add_fusion.1
  87.3 4.0 %dynamic_update_slice.10 = bf16[576,2048]{1,0:T(8,128)(2,1)S(1)} dynamic-update-slice(bf16[576,2048]{1,0:T(8,128)(2,1)S(1)} %dynamic_update_slice.9, bf16[192,2048]{1,0:T(8,128)(2,1)S(1)} %dynamic-slice_add_fusion.1, s32[]{:T(128)S(6)} %select_n.190, s32[]{:T(128)} %constant.48.clone.1) | dynamic-update-slice | bytes 1572868 | tf_op jit(solution)/shard_map/dynamic_update_slice | solution.py:93
  91.4 0.0 collective-permute-done.3
  91.4 1.4 dynamic-slice_add_fusion
  92.8 4.0 %dynamic_update_slice.11 = bf16[576,2048]{1,0:T(8,128)(2,1)S(1)} dynamic-update-slice(bf16[576,2048]{1,0:T(8,128)(2,1)S(1)} %dynamic_update_slice.10, bf16[192,2048]{1,0:T(8,128)(2,1)S(1)} %dynamic-slice_add_fusion, s32[]{:T(128)S(6)} %select_n.197, s32[]{:T(128)} %constant.48.clone.1) | dynamic-update-slice | bytes 1572868 | tf_op jit(solution)/shard_map/dynamic_update_slice | solution.py:93
  96.9 0.3 convert_reduce_fusion
  97.2 0.6 fusion.6
  97.7 0.0 all-to-all-done
  97.8 2.2 %shard_map.91 = f32[128,2048]{1,0:T(8,128)} custom-call(bf16[2048,128]{1,0:T(8,128)(2,1)} %bitcast.18.small_ref), custom_call_target="tpu_custom_call" | custom-call | tf_op jit(solution)/shard_map/pallas_call | solution.py:60
  100.0 1.8 fusion.93
  101.8 1.7 fusion.92
  103.6 50.0 %all-gather.2.cloned.1.call-done = bf16[2048,6144]{1,0:T(8,128)(2,1)} async-done(((bf16[32,6144]{1,0:T(8,128)(2,1)}), bf16[2048,6144]{1,0:T(8,128)(2,1)}) %all-gather.2.cloned.1.call-update) | async-done | bytes 25165840 | tf_op jit(solution)/shard_map/all_gather | solution.py:106
  153.6 10.3 %fusion = f32[384,4096]{1,0:T(8,128)S(1)} fusion(bf16[2048,6144]{1,0:T(8,128)(2,1)} %all-gather.2.cloned.1.call-done, f32[2048]{0:T(1024)S(1)} %bitcast.124, f32[384]{0:T(512)S(1)} %add_rsqrt_fusion.1, f32[384]{0:T(512)S(1)} %broadcast_multiply_fusion.1, bf16[576,2048]{1,0:T(8,128)(2,1)S(1)} %dynamic_update_slice.11), kind=kOutput, calls=%fused_computation | convolution fusion | flops 6446383104 | bytes 24653824 | tf_op jit(solution)/shard_map/dot_general | solution.py:73
  163.9 1.0 fusion.13
  164.9 19.7 %fusion.91 = (f32[384]{0:T(512)S(1)}, f32[384,2048]{1,0:T(8,128)S(1)}) fusion(f32[2048]{0:T(1024)S(1)} %bitcast.105, pred[384]{0:T(512)(128)(4,1)S(1)} %get-tuple-element.86, f32[2048]{0:T(1024)S(1)} %bitcast.106, pred[384]{0:T(512)(128)(4,1)S(1)} %get-tuple-element.57, f32[2048]{0:T(1024)S(1)} %bitcast.107, pred[384]{0:T(512)(128)(4,1)S(1)} %get-tuple-element.58, ...), kind=kLoop, calls=%fused_computation.181 | loop fusion | flops 74710656 | bytes 6567040 | tf_op jit(solution)/shard_map/reduce_sum | solution.py:34
  184.6 0.5 multiply_reduce_fusion
  185.1 8.3 %fusion.60 = bf16[1,384,2048]{2,1,0:T(8,128)(2,1)} fusion(bf16[2048,6144]{1,0:T(8,128)(2,1)} %all-gather.2.cloned.1.call-done, f32[384,2048]{1,0:T(8,128)S(1)} %get-tuple-element.18, f32[2048]{0:T(1024)S(1)} %bitcast.123, f32[384]{0:T(512)S(1)} %add_rsqrt_fusion, f32[384]{0:T(512)S(1)} %broadcast_multiply_fusion, bf16[576,2048]{1,0:T(8,128)(2,1)S(1)} %dynamic_update_slice.11), kind=kOutput, calls=%fused_computation.80 | convolution fusion | flops 3229876224 | bytes 14691328 | tf_op jit(solution)/shard_map/dot_general | solution.py:78
  (8 shorter events, 0.0 us)
Async XLA Ops:
  6.5 55.1 %copy-start = (bf16[1,576,2048]{2,1,0:T(8,128)(2,1)S(1)}, bf16[1,576,2048]{2,1,0:T(8,128)(2,1)}, u32[]{:S(2)}) copy-start(bf16[1,576,2048]{2,1,0:T(8,128)(2,1)} %param.9) | copy-start | bytes 7077892
  6.5 147.1 %all-gather.2.cloned.1.call-start = ((), (), s32[]{:S(2)}) async-start(), calls=%async_computation.1 | async-start | bytes 25559040 | tf_op jit(solution)/shard_map/all_gather | solution.py:106
  23.0 74.8 %all-to-all-start = ((bf16[256,8,128]{2,1,0:T(8,128)(2,1)}), bf16[256,8,128]{2,1,0:T(8,128)(2,1)}, u32[]{:S(2)}, u32[]{:S(2)}) async-start(bf16[256,8,128]{2,1,0:T(8,128)(2,1)} %broadcast_in_dim.308), calls=%async_computation | async-start | bytes 1048576 | tf_op jit(solution)/shard_map/all_to_all | solution.py:112
  51.9 23.9 %collective-permute-start = (s32[2]{0:T(128)S(1)}, s32[2]{0:T(128)S(1)}, u32[]{:S(2)}, u32[]{:S(2)}) collective-permute-start(s32[2]{0:T(128)S(1)} %get-tuple-element.91), channel_id=1, source_target_pairs={{0,4},{4,8},{8,12},{12,16},{16,20},{20,24},{24,28},{28,32},{32,36}... | collective-permute-start | bytes 32 | tf_op jit(solution)/shard_map/ppermute | solution.py:19
  53.5 24.2 %collective-permute-start.2 = (s32[2]{0:T(128)S(1)}, s32[2]{0:T(128)S(1)}, u32[]{:S(2)}, u32[]{:S(2)}) collective-permute-start(s32[2]{0:T(128)S(1)} %get-tuple-element.92), channel_id=1, source_target_pairs={{0,252},{4,0},{8,4},{12,8},{16,12},{20,16},{24,20},{28,24},{32,28}... | collective-permute-start | bytes 32 | tf_op jit(solution)/shard_map/ppermute | solution.py:19
  63.6 22.3 %collective-permute-start.1 = (bf16[192,2048]{1,0:T(8,128)(2,1)}, bf16[192,2048]{1,0:T(8,128)(2,1)}, u32[]{:S(2)}, u32[]{:S(2)}) collective-permute-start(bf16[192,2048]{1,0:T(8,128)(2,1)} %get-tuple-element.21), channel_id=1, source_target_pairs={{0,4},{4,8},{8,12},{12,16},{16,20},{20,24},{24,28},{28,32},{32,36}... | collective-permute-start | bytes 2359304 | tf_op jit(solution)/shard_map/ppermute | solution.py:19
  64.7 26.7 %collective-permute-start.3 = (bf16[192,2048]{1,0:T(8,128)(2,1)}, bf16[192,2048]{1,0:T(8,128)(2,1)}, u32[]{:S(2)}, u32[]{:S(2)}) collective-permute-start(bf16[192,2048]{1,0:T(8,128)(2,1)} %get-tuple-element.19), channel_id=1, source_target_pairs={{0,252},{4,0},{8,4},{12,8},{16,12},{20,16},{24,20},{28,24},{32,28}... | collective-permute-start | bytes 2359304 | tf_op jit(solution)/shard_map/ppermute | solution.py:19
Sparse Core Ops, SparseCore 0:
  20.0 133.5 all-gather.1
